TPU v7x, 32 devices: a whole 2x2x4 slice. The times are simulated.
32 devices in a mesh: dp: 8 (over y, x, core), mp: 4 (over z).
Axes of the slice: x: 2, y: 2, z: 4, core: 2. Of those that a mesh axis runs over, the one named last changes fastest.
Arguments:
- tokens_in: bfloat16 [16384, 768], P(('dp', 'mp')), may hold values from -5 to 5
- timesteps: int32 [8], replicated, may hold values from 0 to 999
- lengths: int32 [8], replicated, may hold values from 512 to 2048, as said below
- time_table: bfloat16 [1000, 768], replicated, may hold values from -0.8984375 to 0.8984375
- norm_gains: float32 [2, 768], replicated, may hold values from 0.5 to 1.5
- norm_biases: float32 [2, 768], replicated, may hold values from -0.6 to 0.6
- w_qkv: bfloat16 [3, 768, 768], P(None, 'dp', 'mp'), may hold values from -0.3125 to 0.3125
- qv_bias: float32 [2, 768], replicated, may hold values from -0.42 to 0.42
- w_out: bfloat16 [768, 768], P('mp', 'dp'), may hold values from -0.21875 to 0.21875
- out_bias: float32 [768], replicated, may hold values from -0.6 to 0.6
- w_up: bfloat16 [768, 3072], P('dp', 'mp'), may hold values from -0.21875 to 0.21875
- up_bias: float32 [3072], replicated, may hold values from -0.8 to 0
- w_down: bfloat16 [3072, 768], P('mp', 'dp'), may hold values from -0.109375 to 0.109375
- down_bias: float32 [768], replicated, may hold values from -0.6 to 0.6
- cotangent: bfloat16 [16384, 768], P(('dp', 'mp')), may hold values from -50 to 50
- teacher: bfloat16 [16384, 768], P(('dp', 'mp')), may hold values from -5 to 5
Outputs:
- output: bfloat16 [16384, 768], P(('dp', 'mp'))
- input_grad: float32 [16384, 768], P(('dp', 'mp'))
- table_grad: float32 [1000, 768], replicated
- norm_gain_grad: float32 [2, 768], replicated
- norm_bias_grad: float32 [2, 768], replicated
- w_qkv_grad: float32 [3, 768, 768], P(None, 'dp', 'mp')
- qv_bias_grad: float32 [2, 768], replicated
- w_out_grad: float32 [768, 768], P('mp', 'dp')
- out_bias_grad: float32 [768], replicated
- w_up_grad: float32 [768, 3072], P('dp', 'mp')
- up_bias_grad: float32 [3072], replicated
- w_down_grad: float32 [3072, 768], P('mp', 'dp')
- down_bias_grad: float32 [768], replicated
Inputs may be any that keep to these rules, and one draw needn't show every extreme that they name: Sequence s holds its valid tokens in its first lengths[s] slots and padding after them; some sequence fills all 2048 slots.
All inputs are finite; a program needn't handle non-finite values.
Results may differ from a plain program's by a relative error of at most 0.0095.
The roundings to bfloat16 on the way count: a program that leaves them out, or rounds other values in their place, can miss the bound.
Values may be sent and summed in bfloat16 or wider, within the bound.
No kernel may reach another device: no remote copies, remote signals or barrier semaphores. Data moves between devices by JAX's collectives and lax.ppermute only.
A program may use at most 128 MiB of HBM per device.

v0:
```python
import jax
import jax.numpy as jnp
from jax import lax
from jax.sharding import PartitionSpec as P

D = 768
HEAD_DIM = 64
FF = 3072
MAXLEN = 2048
SEQ_DEV = 1


far_below = -1e30
epsilon = 1e-05


def norm_rows(values, gain_row, shift_row):
    center = values - jnp.mean(values, axis=-1, keepdims=True)
    spread = jnp.mean(center * center, axis=-1, keepdims=True)
    return center * lax.rsqrt(spread + epsilon) * gain_row + shift_row


def gelu_exact(values):
    return jax.nn.gelu(values, approximate=False)


def contract_rows(left_side, right_side):
    return lax.dot_general(
        left_side, right_side, (((0,), (0,)), ((), ())), preferred_element_type=jnp.float32
    )


def contract_cols(left_side, right_side):
    return lax.dot_general(
        left_side, right_side, (((1,), (1,)), ((), ())), preferred_element_type=jnp.float32
    )


def exact_rows(left_side, right_side):
    return lax.dot_general(
        left_side,
        right_side,
        (((0,), (0,)), ((), ())),
        precision=lax.Precision.HIGHEST,
        preferred_element_type=jnp.float32,
    )


def attend_forward(queries, keys_seq, values_seq, length, block_rows, score_scale):
    blocks = queries.shape[0] // block_rows
    key_kept = jnp.arange(keys_seq.shape[0]) < length
    query_blocks = queries.reshape((blocks, block_rows) + queries.shape[1:])

    def one_block(query_block):
        scores = (
            jnp.einsum("qhd,khd->hqk", query_block, keys_seq, preferred_element_type=jnp.float32)
            * score_scale
        )
        scores = jnp.where(key_kept[None, None, :], scores, far_below)
        highest = jnp.max(scores, axis=-1, keepdims=True)
        exp_scores = jnp.exp(scores - highest)
        totals = jnp.sum(exp_scores, axis=-1, keepdims=True)
        prob_low = (exp_scores / totals).astype(jnp.bfloat16)
        mixed_rows = jnp.einsum(
            "hqk,khd->qhd", prob_low, values_seq, preferred_element_type=jnp.float32
        )
        return (mixed_rows, (highest + jnp.log(totals))[..., 0])

    mixed_rows, log_totals = lax.map(one_block, query_blocks)
    return (mixed_rows.reshape(queries.shape), log_totals)


def attend_backward(
    queries, keys_seq, values_seq, grads_out, log_totals, length, block_rows, score_scale
):
    blocks = queries.shape[0] // block_rows
    key_kept = jnp.arange(keys_seq.shape[0]) < length
    query_blocks = queries.reshape((blocks, block_rows) + queries.shape[1:])
    grad_blocks = grads_out.reshape((blocks, block_rows) + grads_out.shape[1:])

    def one_block(carried, inputs):
        key_grad, value_grad = carried
        query_block, grad_block, log_block = inputs
        scores = (
            jnp.einsum("qhd,khd->hqk", query_block, keys_seq, preferred_element_type=jnp.float32)
            * score_scale
        )
        scores = jnp.where(key_kept[None, None, :], scores, far_below)
        prob_rows = jnp.exp(scores - log_block[..., None])
        value_grad = value_grad + jnp.einsum(
            "hqk,qhd->khd",
            prob_rows.astype(jnp.bfloat16),
            grad_block,
            preferred_element_type=jnp.float32,
        )
        prob_grad = jnp.einsum(
            "qhd,khd->hqk", grad_block, values_seq, preferred_element_type=jnp.float32
        )
        score_grad = (
            prob_rows * (prob_grad - jnp.sum(prob_rows * prob_grad, axis=-1, keepdims=True))
        ).astype(jnp.bfloat16)
        query_grad = (
            jnp.einsum("hqk,khd->qhd", score_grad, keys_seq, preferred_element_type=jnp.float32)
            * score_scale
        )
        key_grad = (
            key_grad
            + jnp.einsum(
                "hqk,qhd->khd", score_grad, query_block, preferred_element_type=jnp.float32
            )
            * score_scale
        )
        return ((key_grad, value_grad), query_grad)

    empty_grad = jnp.zeros(keys_seq.shape, jnp.float32)
    (key_grad, value_grad), query_grad = lax.scan(
        one_block, (empty_grad, empty_grad), (query_blocks, grad_blocks, log_totals)
    )
    return (query_grad.reshape(queries.shape), key_grad, value_grad)


def shards(
    tokens_in,
    timesteps,
    lengths,
    time_table,
    norm_gains,
    norm_biases,
    w_qkv,
    qv_bias,
    w_out,
    out_bias,
    w_up,
    up_bias,
    w_down,
    down_bias,
    cotangent,
    teacher,
):
    model_rank = lax.axis_index("mp")
    data_rank = lax.axis_index("dp")
    model_count = lax.axis_size("mp")
    own_rows = tokens_in.shape[0]
    group_rows = own_rows * model_count
    local_width = w_qkv.shape[2]
    local_hidden = w_up.shape[1]
    local_heads = local_width // HEAD_DIM
    block_rows = min(512, MAXLEN)
    score_scale = HEAD_DIM ** (-0.5)
    group_lengths = lax.dynamic_slice_in_dim(lengths, data_rank * SEQ_DEV, SEQ_DEV)
    group_times = lax.dynamic_slice_in_dim(timesteps, data_rank * SEQ_DEV, SEQ_DEV)
    row_index = model_rank * own_rows + jnp.arange(own_rows)
    row_member = (row_index // MAXLEN)[:, None] == jnp.arange(SEQ_DEV)[None, :]
    row_length = jnp.sum(jnp.where(row_member, group_lengths[None, :], 0), axis=1)
    row_time = jnp.sum(jnp.where(row_member, group_times[None, :], 0), axis=1)
    row_valid = row_index % MAXLEN < row_length
    time_onehot = row_time[:, None] == jnp.arange(time_table.shape[0])[None, :]
    table_rows = jnp.dot(
        time_onehot.astype(jnp.bfloat16), time_table, preferred_element_type=jnp.float32
    )
    start_state = tokens_in.astype(jnp.float32) + table_rows
    qkv_weight, out_weight, up_weight, down_weight = (
        lax.all_gather(w_qkv, "dp", axis=1, tiled=True),
        lax.all_gather(w_out, "dp", axis=1, tiled=True),
        lax.all_gather(w_up, "dp", axis=0, tiled=True),
        lax.all_gather(w_down, "dp", axis=1, tiled=True),
    )
    first_norm = norm_rows(start_state, norm_gains[0], norm_biases[0]).astype(jnp.bfloat16)
    first_all = lax.all_gather(first_norm, "mp", axis=0, tiled=True)
    width_start = model_rank * local_width
    local_bias = lax.dynamic_slice_in_dim(qv_bias, width_start, local_width, 1)
    bias_stack = jnp.stack([local_bias[0], jnp.zeros_like(local_bias[0]), local_bias[1]])
    projected = jnp.einsum("gd,cde->cge", first_all, qkv_weight, preferred_element_type=jnp.float32)
    projected = (projected + bias_stack[:, None, :]).astype(jnp.bfloat16)
    heads_all = projected.reshape(3, SEQ_DEV, MAXLEN, local_heads, HEAD_DIM)
    member = 0
    mixed_seq, log_seq = attend_forward(
        heads_all[0, member],
        heads_all[1, member],
        heads_all[2, member],
        group_lengths[member],
        block_rows,
        score_scale,
    )
    mixed_parts = [mixed_seq]
    log_parts = [log_seq]
    attended = jnp.stack(mixed_parts).reshape(group_rows, local_width).astype(jnp.bfloat16)
    attn_sum = lax.psum_scatter(
        jnp.dot(attended, out_weight, preferred_element_type=jnp.float32),
        "mp",
        scatter_dimension=0,
        tiled=True,
    )
    middle_state = start_state + attn_sum + out_bias
    second_norm = norm_rows(middle_state, norm_gains[1], norm_biases[1]).astype(jnp.bfloat16)
    second_all = lax.all_gather(second_norm, "mp", axis=0, tiled=True)
    hidden_start = model_rank * local_hidden
    hidden_pre = jnp.dot(
        second_all, up_weight, preferred_element_type=jnp.float32
    ) + lax.dynamic_slice_in_dim(up_bias, hidden_start, local_hidden)
    hidden_act = gelu_exact(hidden_pre).astype(jnp.bfloat16)
    ffn_sum = lax.psum_scatter(
        jnp.dot(hidden_act, down_weight, preferred_element_type=jnp.float32),
        "mp",
        scatter_dimension=0,
        tiled=True,
    )
    final_state = middle_state + ffn_sum + down_bias
    output = final_state.astype(jnp.bfloat16)
    valid_total = jnp.sum(lengths).astype(jnp.float32)
    loss_weight = lengths.shape[0] * MAXLEN / valid_total
    final_grad = jnp.where(
        row_valid[:, None],
        cotangent.astype(jnp.float32) + loss_weight * (final_state - teacher.astype(jnp.float32)),
        0.0,
    )
    final_low = final_grad.astype(jnp.bfloat16)
    _, gelu_back = jax.vjp(gelu_exact, hidden_pre)
    final_all = lax.all_gather(final_low, "mp", axis=0, tiled=True)
    down_grad_part = contract_rows(hidden_act, final_all)
    act_grad = contract_cols(final_all, down_weight)
    pre_grad = gelu_back(act_grad)[0].astype(jnp.bfloat16)
    up_grad_part = contract_rows(second_all, pre_grad)
    up_bias_part = lax.dynamic_update_slice_in_dim(
        jnp.zeros((FF,), jnp.float32), jnp.sum(pre_grad, axis=0, dtype=jnp.float32), hidden_start, 0
    )
    second_grad = lax.psum_scatter(
        contract_cols(pre_grad, up_weight), "mp", scatter_dimension=0, tiled=True
    )
    _, second_back = jax.vjp(norm_rows, middle_state, norm_gains[1], norm_biases[1])
    middle_part, gain_two, shift_two = second_back(second_grad)
    middle_grad = final_grad + middle_part
    middle_all = lax.all_gather(middle_grad.astype(jnp.bfloat16), "mp", axis=0, tiled=True)
    out_grad_part = contract_rows(attended, middle_all)
    attended_grad = contract_cols(middle_all, out_weight).astype(jnp.bfloat16)
    grad_heads = attended_grad.reshape(SEQ_DEV, MAXLEN, local_heads, HEAD_DIM)
    member = 0
    query_grad, key_grad, value_grad = attend_backward(
        heads_all[0, member],
        heads_all[1, member],
        heads_all[2, member],
        grad_heads[member],
        log_parts[member],
        group_lengths[member],
        block_rows,
        score_scale,
    )
    query_grads = [query_grad]
    key_grads = [key_grad]
    value_grads = [value_grad]
    projected_grad = jnp.stack(
        [jnp.stack(query_grads), jnp.stack(key_grads), jnp.stack(value_grads)]
    )
    projected_grad = projected_grad.reshape(3, group_rows, local_width).astype(jnp.bfloat16)
    qkv_grad_part = jnp.einsum(
        "gd,cge->cde", first_all, projected_grad, preferred_element_type=jnp.float32
    )
    bias_sums = jnp.sum(projected_grad, axis=1, dtype=jnp.float32)
    qv_bias_part = lax.dynamic_update_slice_in_dim(
        jnp.zeros((2, D), jnp.float32), jnp.stack([bias_sums[0], bias_sums[2]]), width_start, 1
    )
    first_grad = lax.psum_scatter(
        jnp.einsum("cge,cde->gd", projected_grad, qkv_weight, preferred_element_type=jnp.float32),
        "mp",
        scatter_dimension=0,
        tiled=True,
    )
    _, first_back = jax.vjp(norm_rows, start_state, norm_gains[0], norm_biases[0])
    start_part, gain_one, shift_one = first_back(first_grad)
    input_grad = middle_grad + start_part
    qkv_grad, out_grad, up_grad, down_grad = (
        lax.psum_scatter(qkv_grad_part, "dp", scatter_dimension=1, tiled=True),
        lax.psum_scatter(out_grad_part, "dp", scatter_dimension=1, tiled=True),
        lax.psum_scatter(up_grad_part, "dp", scatter_dimension=0, tiled=True),
        lax.psum_scatter(down_grad_part, "dp", scatter_dimension=1, tiled=True),
    )
    vector_part = jnp.stack(
        [
            gain_one,
            gain_two,
            shift_one,
            shift_two,
            qv_bias_part[0],
            qv_bias_part[1],
            jnp.sum(middle_grad, axis=0),
            jnp.sum(final_grad, axis=0),
        ]
    )
    table_part = exact_rows(time_onehot.astype(jnp.float32), input_grad)
    vector_sum, up_bias_grad, table_grad = lax.psum(
        (vector_part, up_bias_part, table_part), ("dp", "mp")
    )
    return (
        output,
        input_grad,
        table_grad,
        vector_sum[0:2],
        vector_sum[2:4],
        qkv_grad,
        vector_sum[4:6],
        out_grad,
        vector_sum[6],
        up_grad,
        up_bias_grad,
        down_grad,
        vector_sum[7],
    )


def solution(mesh):
    placed = (
        P(("dp", "mp"), None),
        P(),
        P(),
        P(),
        P(),
        P(),
        P(None, "dp", "mp"),
        P(),
        P("mp", "dp"),
        P(),
        P("dp", "mp"),
        P(),
        P("mp", "dp"),
        P(),
        P(("dp", "mp"), None),
        P(("dp", "mp"), None),
    )
    return jax.shard_map(
        shards,
        mesh=mesh,
        in_specs=placed,
        out_specs=(
            P(("dp", "mp"), None),
            P(("dp", "mp"), None),
            P(),
            P(),
            P(),
            P(None, "dp", "mp"),
            P(),
            P("mp", "dp"),
            P(),
            P("dp", "mp"),
            P(),
            P("mp", "dp"),
            P(),
        ),
        check_vma=False,
    )
```

profile of v0, /device:TPU:0, one launch (start us, length us, event | category | flops | bytes accessed | tf_op | source)
XLA Modules:
  0.0 1150.8 jit_solution(8117117334112619755)
XLA Ops:
  17.3 14.6 %all_gather.25 = bf16[3,768,192]{2,0,1:T(4,128)(2,1)S(1)} all-gather(bf16[3,96,192]{2,0,1:T(4,128)(2,1)S(1)} %copy.44), channel_id=1, replica_groups=mesh['dp'=8,'mp'=4] {'dp'}, dimensions={1}, use_global_device_ids=true | all-gather | bytes 995328 | tf_op jit(solution)/shard_map/all_gather | solution.py:163
  34.1 8.7 all_gather.26
  43.7 39.0 %all-gather.7.cloned.1.call-done = bf16[2048,768]{1,0:T(8,128)(2,1)} async-done(((bf16[512,768]{1,0:T(8,128)(2,1)}), bf16[2048,768]{1,0:T(8,128)(2,1)}) %all-gather.7.cloned.1.call-update) | async-done | bytes 3145744 | tf_op jit(solution)/shard_map/all_gather | solution.py:169
  91.1 40.3 %while.28 = (s32[]{:T(128)}, bf16[4,512,3,64]{1,3,2,0:T(8,128)(2,1)}, f32[4,3,512]{2,1,0:T(4,128)S(1)}, bf16[4,512,3,64]{1,3,2,0:T(8,128)(2,1)S(1)}, bf16[2048,3...) while((s32[]{:T(128)}, ...), condition=%wide.region_5.6_spmd.clone, body=%wide.region_2.5_spmd.clone.sunk | while | flops 843055616 | bytes 46270628 | solution.py:69
  139.1 108.9 %reduce-scatter.13.cloned.1.call-done = f32[512,768]{1,0:T(8,128)} async-done(((f32[2048,768]{1,0:T(8,128)}), f32[512,768]{1,0:T(8,128)}) %reduce-scatter.13.cloned.1.call-update) | async-done | bytes 1572880 | tf_op jit(solution)/shard_map/reduce_scatter | solution.py:188
  253.4 62.4 %all-gather.9.cloned.1.call-done = bf16[2048,768]{1,0:T(8,128)(2,1)} async-done(((bf16[512,768]{1,0:T(8,128)(2,1)}), bf16[2048,768]{1,0:T(8,128)(2,1)}) %all-gather.9.cloned.1.call-update) | async-done | bytes 3145744 | tf_op jit(solution)/shard_map/all_gather | solution.py:196
  315.7 18.9 %multiply_convert_fusion.1 = (bf16[2048,768]{1,0:T(8,128)(2,1)}, f32[2048,768]{1,0:T(8,128)}, f32[2048,768]{1,0:T(8,128)}) fusion(f32[768]{0:T(1024)S(1)} %dynamic_slice.29, bf16[2048,768]{1,0:T(8,128)(2,1)} %all-gather.9.cloned.1.call-done, bf16[768,768]{1,0:T(8,128)(2,1)} %all-gather.11.cloned.1.call-done), kind=kOutput, calls=%fused_computation.54 | convolution fusion | flops 2519728128 | bytes 20057088 | tf_op jit(solution)/shard_map/dot_general | solution.py:198
  340.1 7.5 fusion.81
  350.2 108.2 %reduce-scatter.15.cloned.1.call-done = f32[512,768]{1,0:T(8,128)} async-done(((f32[2048,768]{1,0:T(8,128)}), f32[512,768]{1,0:T(8,128)}) %reduce-scatter.15.cloned.1.call-update) | async-done | bytes 1572880 | tf_op jit(solution)/shard_map/reduce_scatter | solution.py:202
  464.8 63.7 %all-gather.15.cloned.1.call-done = bf16[2048,768]{1,0:T(8,128)(2,1)} async-done(((bf16[512,768]{1,0:T(8,128)(2,1)}), bf16[2048,768]{1,0:T(8,128)(2,1)}) %all-gather.15.cloned.1.call-update) | async-done | bytes 3145744 | tf_op jit(solution)/shard_map/all_gather | solution.py:219
  528.5 11.1 convert_reduce_fusion
  545.9 109.4 %reduce-scatter.17.cloned.1.call-done = f32[512,768]{1,0:T(8,128)} async-done(((f32[2048,768]{1,0:T(8,128)}), f32[512,768]{1,0:T(8,128)}) %reduce-scatter.17.cloned.1.call-update) | async-done | bytes 1572880 | tf_op jit(solution)/shard_map/reduce_scatter | solution.py:227
  662.5 64.1 %all-gather.17.cloned.1.call-done = bf16[2048,768]{1,0:T(8,128)(2,1)} async-done(((bf16[512,768]{1,0:T(8,128)(2,1)}), bf16[2048,768]{1,0:T(8,128)(2,1)}) %all-gather.17.cloned.1.call-update) | async-done | bytes 3145744 | tf_op jit(solution)/shard_map/all_gather | solution.py:233
  736.7 105.6 %while.29 = (s32[]{:T(128)}, f32[2048,3,64]{0,2,1:T(8,128)S(1)}, f32[2048,3,64]{0,2,1:T(8,128)}, bf16[4,512,3,64]{1,3,2,0:T(8,128)(2,1)}, bf16[4,512,3,64]{1,3,2...) while((s32[]{:T(128)}, f32[2048,3,64]{0,2,1:T(8,128)S(1)}, ...), condition=%wide.region_16.17_spmd.clone, body=%wide.region_14.16_spmd.clone.sunk | while | flops 2062516736 | bytes 129419448 | solution.py:116
  781.2 5.6 fusion.150
  834.1 5.6 fusion.150
  858.4 5.7 fusion.56
  873.0 6.9 fusion.83
  880.2 6.9 fusion.84
  887.2 75.4 %reduce-scatter.19.cloned.1.call-done = f32[512,768]{1,0:T(8,128)} async-done(((f32[2048,768]{1,0:T(8,128)}), f32[512,768]{1,0:T(8,128)}) %reduce-scatter.19.cloned.1.call-update) | async-done | bytes 1572880 | tf_op jit(solution)/shard_map/reduce_scatter | solution.py:262
  973.6 28.2 %reduce-scatter.27.cloned.1.call-done = f32[96,192]{1,0:T(8,128)} async-done(((f32[768,192]{1,0:T(8,128)}), f32[96,192]{1,0:T(8,128)}) %reduce-scatter.27.cloned.1.call-update) | async-done | bytes 73744
  1003.4 42.7 %reduce-scatter.25.cloned.1.call-done = f32[96,576]{1,0:T(8,128)} async-done(((f32[768,576]{1,0:T(8,128)}), f32[96,576]{1,0:T(8,128)}) %reduce-scatter.25.cloned.1.call-update) | async-done | bytes 221200
  1048.1 40.7 %all-reduce = (f32[8,768]{1,0:T(8,128)S(1)}, f32[3072]{0:T(1024)}) all-reduce(f32[8,768]{1,0:T(8,128)S(1)} %stack.37, f32[3072]{0:T(1024)S(1)} %dynamic_update_slice.18), channel_id=1, replica_groups=mesh['dp'=8,'mp'=4] {'dp','mp'}, use_global_device_ids=true, to_apply=%region_28.29 | all-reduce | flops 9216 | bytes 73728 | tf_op jit(solution)/shard_map/psum | solution.py:290
  1092.9 46.9 %reduce-scatter.23.cloned.1.call-done = f32[768,96]{0,1:T(8,128)} async-done(((f32[768,768]{0,1:T(8,128)}), f32[768,96]{0,1:T(8,128)}) %reduce-scatter.23.cloned.1.call-update) | async-done | bytes 294928 | tf_op jit(solution)/shard_map/reduce_scatter | solution.py:275
  (281 shorter events, 252.1 us)
Async XLA Ops:
  8.0 74.7 %all-gather.7.cloned.1.call-start = ((), (), s32[]{:S(2)}) async-start(), calls=%async_computation.8 | async-start | bytes 3932160 | tf_op jit(solution)/shard_map/all_gather | solution.py:169
  16.3 231.7 %reduce-scatter.13.cloned.1.call-start = ((), (), s32[]{:S(2)}) async-start(), calls=%async_computation.9 | async-start | bytes 7864320 | tf_op jit(solution)/shard_map/reduce_scatter | solution.py:188
  138.5 109.6 %copy-start.41 = (f32[768]{0:T(1024)S(1)}, f32[768]{0:T(1024)}, u32[]{:S(2)}) copy-start(f32[768]{0:T(1024)} %param.29) | copy-start | bytes 9220
  138.5 114.9 %all-gather.11.cloned.1.call-start = ((), (), s32[]{:S(2)}) async-start(), calls=%async_computation.11 | async-start | bytes 1327104 | tf_op jit(solution)/shard_map/all_gather | solution.py:165
  139.1 176.7 %all-gather.9.cloned.1.call-start = ((), (), s32[]{:S(2)}) async-start(), calls=%async_computation.10 | async-start | bytes 3932160 | tf_op jit(solution)/shard_map/all_gather | solution.py:196
  251.8 88.3 %all-gather.13.cloned.1.call-start = ((), (), s32[]{:S(2)}) async-start(), calls=%async_computation.12 | async-start | bytes 1327104 | tf_op jit(solution)/shard_map/all_gather | solution.py:166
  252.3 206.0 %reduce-scatter.15.cloned.1.call-start = ((), (), s32[]{:S(2)}) async-start(), calls=%async_computation.13 | async-start | bytes 7864320 | tf_op jit(solution)/shard_map/reduce_scatter | solution.py:202
  347.5 110.8 %copy-start.42 = (f32[768]{0:T(1024)S(1)}, f32[768]{0:T(1024)}, u32[]{:S(2)}) copy-start(f32[768]{0:T(1024)} %param.33) | copy-start | bytes 9220
  347.6 180.9 %all-gather.15.cloned.1.call-start = ((), (), s32[]{:S(2)}) async-start(), calls=%async_computation.14 | async-start | bytes 3932160 | tf_op jit(solution)/shard_map/all_gather | solution.py:219
  464.3 190.9 %reduce-scatter.17.cloned.1.call-start = ((), (), s32[]{:S(2)}) async-start(), calls=%async_computation.15 | async-start | bytes 7864320 | tf_op jit(solution)/shard_map/reduce_scatter | solution.py:227
  528.5 12.8 %copy-start.44 = (bf16[768,768]{1,0:T(8,128)(2,1)S(1)}, bf16[768,768]{1,0:T(8,128)(2,1)}, u32[]{:S(2)}) copy-start(bf16[768,768]{1,0:T(8,128)(2,1)} %all-gather.11.cloned.1.call-done) | copy-start | bytes 3538948
  545.8 180.8 %all-gather.17.cloned.1.call-start = ((), (), s32[]{:S(2)}) async-start(), calls=%async_computation.16 | async-start | bytes 3932160 | tf_op jit(solution)/shard_map/all_gather | solution.py:233
  662.4 300.2 %reduce-scatter.19.cloned.1.call-start = ((), (), s32[]{:S(2)}) async-start(), calls=%async_computation.17 | async-start | bytes 7864320 | tf_op jit(solution)/shard_map/reduce_scatter | solution.py:262
  853.0 148.7 %reduce-scatter.27.cloned.1.call-start = ((), (), s32[]{:S(2)}) async-start(), calls=%async_computation.22 | async-start | bytes 884736
  858.3 187.8 %reduce-scatter.25.cloned.1.call-start = ((), (), s32[]{:S(2)}) async-start(), calls=%async_computation.21 | async-start | bytes 2211840
  872.9 219.9 %reduce-scatter.21.cloned.1.call-start = ((), (), s32[]{:S(2)}) async-start(), calls=%async_computation.19 | async-start | bytes 2654208 | tf_op jit(solution)/shard_map/reduce_scatter | solution.py:274
  879.9 82.7 %copy-start.27 = (f32[768]{0:T(1024)S(1)}, f32[768]{0:T(1024)}, u32[]{:S(2)}) copy-start(f32[768]{0:T(1024)} %copy-done.26) | copy-start | bytes 9220
  879.9 82.7 %copy-start.29 = (f32[512]{0:T(512)S(1)}, f32[512]{0:T(512)}, u32[]{:S(2)}) copy-start(f32[512]{0:T(512)} %copy-done.28) | copy-start | bytes 6148
  879.9 82.7 %copy-start.32 = (f32[512]{0:T(512)S(1)}, f32[512]{0:T(512)}, u32[]{:S(2)}) copy-start(f32[512]{0:T(512)} %copy-done.31) | copy-start | bytes 6148
  879.9 259.8 %reduce-scatter.23.cloned.1.call-start = ((), (), s32[]{:S(2)}) async-start(), calls=%async_computation.20 | async-start | bytes 2654208 | tf_op jit(solution)/shard_map/reduce_scatter | solution.py:275
  887.1 75.5 %copy-start.5 = (f32[512,768]{1,0:T(8,128)S(1)}, f32[512,768]{1,0:T(8,128)}, u32[]{:S(2)}) copy-start(f32[512,768]{1,0:T(8,128)} %copy-done.4) | copy-start | bytes 4718596
  887.1 77.7 %copy-start.34 = (f32[512]{0:T(512)S(1)}, f32[512]{0:T(512)}, u32[]{:S(2)}) copy-start(f32[512]{0:T(512)} %copy-done.33) | copy-start | bytes 6148
  887.2 252.6 %all-reduce.3.cloned.1.call-start = ((), (), s32[]{:S(2)}) async-start(), calls=%async_computation.18 | async-start | bytes 6144000 | tf_op jit(solution)/shard_map/psum | solution.py:290
  1048.0 95.4 %copy-start.1 = (bf16[1000,768]{1,0:T(8,128)(2,1)S(1)}, bf16[1000,768]{1,0:T(8,128)(2,1)}, u32[]{:S(2)}) copy-start(bf16[1000,768]{1,0:T(8,128)(2,1)} %param.23) | copy-start | bytes 4608004
  (48 other events, 148.9 us)
Sparse Core Ops, SparseCore 0:
  16.4 66.1 all-gather.6
  138.6 109.3 reduce-scatter.12
  464.4 63.9 all-gather.14
  662.5 64.0 all-gather.16
  853.2 109.3 reduce-scatter.18
  965.9 35.8 reduce-scatter.26
  1005.5 40.5 reduce-scatter.24
  1050.0 42.7 reduce-scatter.20
  1097.2 42.5 reduce-scatter.22
Sparse Core Ops, SparseCore 1:
  140.9 22.5 all-gather.10
  251.8 63.8 all-gather.8
  317.5 22.5 all-gather.12
  347.6 110.6 reduce-scatter.14
  545.9 109.3 reduce-scatter.16
  971.3 144.0 all-reduce.2
where the time goes:
time: 1160 us; the launch traced here: 1150 us
  waiting for transfers between devices  758 us (65%)
  matrix products  195 us (17%)
  blocking collectives  64 us (6%)
  other arithmetic  60.3 us (5%)
  local copies, waits for them, and re-layouts  54.3 us (5%)
  between operations  17 us (1%)
    reduce_scatter x1, waiting for transfers between devices, shards(): lax.psum_scatter(contract_cols(pre_grad, up_weight), 'mp', scatter_dimens...  109 us
    reduce_scatter x1, waiting for transfers between devices, shards(): lax.psum_scatter(jnp.dot(attended, out_weight, preferred_element_type=jnp...  109 us
    reduce_scatter x1, waiting for transfers between devices, shards(): lax.psum_scatter(jnp.dot(hidden_act, down_weight, preferred_element_type=...  108 us
    reduce_scatter x1, waiting for transfers between devices, shards(): lax.psum_scatter(jnp.einsum('cge,cde->gd', projected_grad, qkv_weight, pr...  75.4 us
    unnamed x17, waiting for transfers between devices  72.2 us
    all_gather x1, waiting for transfers between devices, shards(): lax.all_gather(middle_grad.astype(jnp.bfloat16), 'mp', axis=0, tiled=True)  64.1 us
    all_gather x1, waiting for transfers between devices, shards(): final_all = lax.all_gather(final_low, 'mp', axis=0, tiled=True)  63.7 us
    all_gather x1, waiting for transfers between devices, shards(): second_all = lax.all_gather(second_norm, 'mp', axis=0, tiled=True)  62.4 us
  transfers between devices with their start and end apart: 15, of which 13 were waited for; matrix products, arithmetic and copies ran while one was open for 7% of the time, Pallas kernels for 0%

commit v1 on v0

v1 whole, which is shorter than its diff:
```python
import functools

import jax
import jax.numpy as jnp
from jax import lax
from jax.experimental import pallas as pl
from jax.experimental.pallas import tpu as pltpu
from jax.sharding import PartitionSpec as P

D = 768
HEADS = 12
HEAD_DIM = 64
FF = 3072
MAXLEN = 2048
PAIR = 2 * HEAD_DIM
PAIRS = HEADS // 2
KEY_BLOCK = 512

far_below = -1e30
epsilon = 1e-05
score_scale = HEAD_DIM ** (-0.5)
low = jnp.bfloat16
full = jnp.float32
both = ("dp", "mp")


def norm_stats(values):
    center = values - jnp.mean(values, axis=-1, keepdims=True)
    spread = jnp.mean(center * center, axis=-1, keepdims=True)
    inverse = lax.rsqrt(spread + epsilon)
    return center * inverse, inverse


def norm_back(unit, inverse, gain_row, grad):
    scaled = grad * gain_row
    mean_scaled = jnp.mean(scaled, axis=-1, keepdims=True)
    mean_unit = jnp.mean(scaled * unit, axis=-1, keepdims=True)
    return (
        inverse * (scaled - mean_scaled - unit * mean_unit),
        jnp.sum(grad * unit, axis=0),
        jnp.sum(grad, axis=0),
    )


def dot_of(left_side, right_side, left_dim, right_dim):
    return lax.dot_general(
        left_side,
        right_side,
        (((left_dim,), (right_dim,)), ((), ())),
        preferred_element_type=full,
    )


def first_half(shape):
    return lax.broadcasted_iota(jnp.int32, shape, len(shape) - 1) < HEAD_DIM


def forward_kernel(length_ref, q_ref, k_ref, v_ref, out_ref, log_ref):
    rows = q_ref.shape[0]
    keys = k_ref.shape[0]
    length = length_ref[0]
    bias = jnp.where(
        lax.broadcasted_iota(jnp.int32, (1, keys), 1) < length, 0.0, far_below
    )
    q_pair = q_ref[...]
    k_pair = k_ref[...]
    v_pair = v_ref[...]
    lower = first_half((rows, PAIR))
    mixed = []
    logs = []
    for half in range(2):
        kept = lower if half == 0 else jnp.logical_not(lower)
        q_half = jnp.where(kept, q_pair, jnp.zeros_like(q_pair))
        scores = dot_of(q_half, k_pair, 1, 1) + bias
        highest = jnp.max(scores, axis=-1, keepdims=True)
        exp_scores = jnp.exp(scores - highest)
        totals = jnp.sum(exp_scores, axis=-1, keepdims=True)
        mixed.append(dot_of(exp_scores.astype(low), v_pair, 1, 0) / totals)
        logs.append(highest + jnp.log(totals))
    out_ref[...] = jnp.where(lower, mixed[0], mixed[1])
    lane = lax.broadcasted_iota(jnp.int32, (rows, PAIR), 1)
    log_ref[...] = jnp.where(lower, logs[0], logs[1])


def attend_forward(queries, keys, values, length):
    rows, total = queries.shape[0], keys.shape[0]
    pair_rows = lambda count: pl.BlockSpec((count, PAIR), lambda i, n: (0, i))
    return pl.pallas_call(
        forward_kernel,
        out_shape=(
            jax.ShapeDtypeStruct((rows, D), full),
            jax.ShapeDtypeStruct((rows, D), full),
        ),
        grid_spec=pltpu.PrefetchScalarGridSpec(
            num_scalar_prefetch=1,
            grid=(PAIRS,),
            in_specs=[pair_rows(rows), pair_rows(total), pair_rows(total)],
            out_specs=[pair_rows(rows), pair_rows(rows)],
        ),
        compiler_params=pltpu.CompilerParams(vmem_limit_bytes=56 << 20),
        cost_estimate=pl.CostEstimate(
            flops=4 * rows * total * D * 4,
            bytes_accessed=12 * total * D,
            transcendentals=rows * total * HEADS,
        ),
        name="attend_forward",
    )(length, queries, keys, values)


def backward_kernel(
    length_ref, q_ref, k_ref, v_ref, g_ref, log_ref, delta_ref, dq_ref, dk_ref, dv_ref
):
    rows = q_ref.shape[0]
    keys = k_ref.shape[0]
    length = length_ref[0]
    q_pair = q_ref[...]
    g_pair = g_ref[...]
    lower = first_half((rows, PAIR))
    lower_keys = first_half((KEY_BLOCK, PAIR))
    dq = [jnp.zeros((rows, PAIR), full), jnp.zeros((rows, PAIR), full)]
    for block in range(keys // KEY_BLOCK):
        span = slice(block * KEY_BLOCK, (block + 1) * KEY_BLOCK)
        k_pair = k_ref[span, :]
        v_pair = v_ref[span, :]
        place = block * KEY_BLOCK + lax.broadcasted_iota(
            jnp.int32, (KEY_BLOCK, 1), 0
        )
        bias = jnp.where(place < length, 0.0, far_below)
        dk = []
        dv = []
        for half in range(2):
            kept = lower if half == 0 else jnp.logical_not(lower)
            q_half = jnp.where(kept, q_pair, jnp.zeros_like(q_pair))
            g_half = jnp.where(kept, g_pair, jnp.zeros_like(g_pair))
            log_row = log_ref[0, half : half + 1, :]
            delta_row = delta_ref[0, half : half + 1, :]
            scores = dot_of(k_pair, q_half, 1, 1) + bias
            probs = jnp.exp(scores - log_row)
            dv.append(dot_of(probs.astype(low), g_pair, 1, 0))
            prob_grad = dot_of(v_pair, g_half, 1, 1)
            score_grad = (probs * (prob_grad - delta_row)).astype(low)
            dk.append(dot_of(score_grad, q_pair, 1, 0))
            dq[half] = dq[half] + dot_of(score_grad, k_pair, 0, 0)
        dk_ref[span, :] = jnp.where(lower_keys, dk[0], dk[1]).astype(low)
        dv_ref[span, :] = jnp.where(lower_keys, dv[0], dv[1]).astype(low)
    dq_ref[...] = (jnp.where(lower, dq[0], dq[1]) * score_scale).astype(low)


def attend_backward(queries, keys, values, grads, logs, deltas, length):
    rows, total = queries.shape[0], keys.shape[0]
    pair_rows = lambda count: pl.BlockSpec((count, PAIR), lambda i, n: (0, i))
    stats = pl.BlockSpec((1, 2, rows), lambda i, n: (i, 0, 0))
    return pl.pallas_call(
        backward_kernel,
        out_shape=(
            jax.ShapeDtypeStruct((rows, D), low),
            jax.ShapeDtypeStruct((total, D), low),
            jax.ShapeDtypeStruct((total, D), low),
        ),
        grid_spec=pltpu.PrefetchScalarGridSpec(
            num_scalar_prefetch=1,
            grid=(PAIRS,),
            in_specs=[
                pair_rows(rows),
                pair_rows(total),
                pair_rows(total),
                pair_rows(rows),
                stats,
                stats,
            ],
            out_specs=[pair_rows(rows), pair_rows(total), pair_rows(total)],
        ),
        compiler_params=pltpu.CompilerParams(vmem_limit_bytes=56 << 20),
        cost_estimate=pl.CostEstimate(
            flops=10 * rows * total * D * 4,
            bytes_accessed=16 * total * D,
            transcendentals=rows * total * HEADS,
        ),
        name="attend_backward",
    )(length, queries, keys, values, grads, logs, deltas)


def shards(
    tokens_in,
    timesteps,
    lengths,
    time_table,
    norm_gains,
    norm_biases,
    w_qkv,
    qv_bias,
    w_out,
    out_bias,
    w_up,
    up_bias,
    w_down,
    down_bias,
    cotangent,
    teacher,
):
    model_rank = lax.axis_index("mp")
    data_rank = lax.axis_index("dp")
    mp = lax.axis_size("mp")
    dp = lax.axis_size("dp")
    own_rows = tokens_in.shape[0]
    length = lax.dynamic_slice_in_dim(lengths, data_rank, 1)
    own_time = lax.dynamic_slice_in_dim(timesteps, data_rank, 1)
    position = model_rank * own_rows + jnp.arange(own_rows)
    row_valid = position < length[0]
    table_row = lax.dynamic_slice_in_dim(time_table, own_time[0], 1)
    start_state = tokens_in.astype(full) + table_row.astype(full)

    gather_all = functools.partial(lax.all_gather, axis_name=("mp", "dp"), axis=0, tiled=True)
    qkv_weight = lax.all_gather(w_qkv, "mp", axis=2, tiled=True)
    qkv_weight = lax.all_gather(qkv_weight, "dp", axis=1, tiled=True)
    up_weight = gather_all(w_up).reshape(mp, D, -1)
    down_weight = gather_all(w_down.T).reshape(mp, D, -1)
    out_weight = lax.all_gather(w_out, "dp", axis=1, tiled=True)
    out_weight = lax.all_gather(out_weight, "mp", axis=0, tiled=True)

    unit_one, inverse_one = norm_stats(start_state)
    first_norm = (unit_one * norm_gains[0] + norm_biases[0]).astype(low)
    first_all = lax.all_gather(first_norm, "mp", axis=0, tiled=True)

    queries = ((dot_of(first_norm, qkv_weight[0], 1, 0) + qv_bias[0]).astype(low) * score_scale).astype(low)
    keys = dot_of(first_all, qkv_weight[1], 1, 0).astype(low)
    values = (dot_of(first_all, qkv_weight[2], 1, 0) + qv_bias[1]).astype(low)
    mixed, logs = attend_forward(queries, keys, values, length)
    attended = mixed.astype(low)

    middle_state = start_state + dot_of(attended, out_weight, 1, 0) + out_bias
    unit_two, inverse_two = norm_stats(middle_state)
    second_norm = (unit_two * norm_gains[1] + norm_biases[1]).astype(low)
    hidden_pre = jnp.einsum(
        "td,mdf->mtf", second_norm, up_weight, preferred_element_type=full
    ) + up_bias.reshape(mp, 1, -1)
    error = lax.erf(hidden_pre * (0.5**0.5))
    cumulative = 0.5 * (1.0 + error)
    hidden_act = (hidden_pre * cumulative).astype(low)
    act_slope = cumulative + hidden_pre * jnp.exp(-0.5 * hidden_pre * hidden_pre) * (
        (2.0 * jnp.pi) ** -0.5
    )
    final_state = (
        middle_state
        + jnp.einsum("mtf,mdf->td", hidden_act, down_weight, preferred_element_type=full)
        + down_bias
    )
    output = final_state.astype(low)
    loss_weight = lengths.shape[0] * MAXLEN / jnp.sum(lengths).astype(full)
    final_grad = jnp.where(
        row_valid[:, None],
        cotangent.astype(full) + loss_weight * (final_state - teacher.astype(full)),
        0.0,
    )
    final_low = final_grad.astype(low)
    down_part = jnp.einsum(
        "td,mtf->mdf", final_low, hidden_act, preferred_element_type=full
    )
    act_grad = jnp.einsum("td,mdf->mtf", final_low, down_weight, preferred_element_type=full)
    pre_grad = (act_slope * act_grad).astype(low)
    up_part = jnp.einsum("td,mtf->mdf", second_norm, pre_grad, preferred_element_type=full)
    up_bias_part = jnp.sum(pre_grad, axis=1, dtype=full).reshape(FF)
    second_grad = jnp.einsum("mtf,mdf->td", pre_grad, up_weight, preferred_element_type=full)
    middle_part, gain_two, shift_two = norm_back(
        unit_two, inverse_two, norm_gains[1], second_grad
    )
    middle_grad = final_grad + middle_part
    middle_low = middle_grad.astype(low)
    out_part = dot_of(middle_low, attended, 0, 0)
    attended_grad = dot_of(middle_low, out_weight, 1, 1).astype(low)

    scatter_all = functools.partial(
        lax.psum_scatter, axis_name=("mp", "dp"), scatter_dimension=0, tiled=True
    )
    down_grad = scatter_all(down_part.astype(low).reshape(mp * D, -1)).astype(full).T
    up_grad = scatter_all(up_part.astype(low).reshape(mp * D, -1)).astype(full)

    deltas = jnp.sum(
        (attended_grad.astype(full) * mixed).reshape(own_rows, HEADS, HEAD_DIM), axis=-1
    )
    deltas = deltas.T.reshape(PAIRS, 2, own_rows)
    logs = logs.reshape(own_rows, HEADS, HEAD_DIM)[:, :, 0].T.reshape(PAIRS, 2, own_rows)
    query_grad, key_grad, value_grad = attend_backward(
        queries, keys, values, attended_grad, logs, deltas, length
    )
    first_part = dot_of(key_grad, qkv_weight[1], 1, 1) + dot_of(value_grad, qkv_weight[2], 1, 1)
    first_query = dot_of(query_grad, qkv_weight[0], 1, 1)
    first_grad = first_query + lax.psum_scatter(
        first_part.astype(low), "mp", scatter_dimension=0, tiled=True
    ).astype(full)
    qkv_part = jnp.stack(
        [
            dot_of(first_norm, query_grad, 0, 0),
            dot_of(first_all, key_grad, 0, 0),
            dot_of(first_all, value_grad, 0, 0),
        ]
    ).astype(low)
    qv_bias_part = jnp.stack(
        [jnp.sum(query_grad, axis=0, dtype=full), jnp.sum(value_grad, axis=0, dtype=full)]
    )
    qkv_grad = lax.psum_scatter(qkv_part, "mp", scatter_dimension=2, tiled=True)
    qkv_grad = lax.psum_scatter(qkv_grad, "dp", scatter_dimension=1, tiled=True).astype(full)
    out_grad = lax.psum_scatter(out_part.T.astype(low), "mp", scatter_dimension=0, tiled=True)
    out_grad = lax.psum_scatter(out_grad, "dp", scatter_dimension=1, tiled=True).astype(full)

    start_part, gain_one, shift_one = norm_back(
        unit_one, inverse_one, norm_gains[0], first_grad
    )
    input_grad = middle_grad + start_part
    sequence_sum = jnp.sum(input_grad, axis=0)
    own_slot = (jnp.arange(dp) == data_rank).astype(full)
    packed = jnp.concatenate(
        [
            jnp.stack([gain_one, gain_two, shift_one, shift_two]),
            qv_bias_part,
            jnp.stack([jnp.sum(middle_grad, axis=0), jnp.sum(final_grad, axis=0)]),
            up_bias_part.reshape(-1, D),
            own_slot[:, None] * sequence_sum[None, :],
        ]
    )
    total = lax.psum(packed, both)
    fixed = 8 + FF // D
    chosen = (timesteps[None, :] == jnp.arange(time_table.shape[0])[:, None]).astype(full)
    table_grad = lax.dot_general(
        chosen,
        total[fixed:],
        (((1,), (0,)), ((), ())),
        precision=lax.Precision.HIGHEST,
        preferred_element_type=full,
    )
    return (
        output,
        input_grad,
        table_grad,
        total[0:2],
        total[2:4],
        qkv_grad,
        total[4:6],
        out_grad,
        total[6],
        up_grad,
        total[8:fixed].reshape(FF),
        down_grad,
        total[7],
    )


def solution(mesh):
    rows = P(both, None)
    placed = (
        rows,
        P(),
        P(),
        P(),
        P(),
        P(),
        P(None, "dp", "mp"),
        P(),
        P("mp", "dp"),
        P(),
        P("dp", "mp"),
        P(),
        P("mp", "dp"),
        P(),
        rows,
        rows,
    )
    return jax.shard_map(
        shards,
        mesh=mesh,
        in_specs=placed,
        out_specs=(
            rows,
            rows,
            P(),
            P(),
            P(),
            P(None, "dp", "mp"),
            P(),
            P("mp", "dp"),
            P(),
            P("dp", "mp"),
            P(),
            P("mp", "dp"),
            P(),
        ),
        check_vma=False,
    )
```

time: 1160 us -> 813 us (0.70)
  waiting for transfers between devices: 758 us -> 494 us
  matrix products: 195 us -> 94.4 us
  Pallas kernels: 0 us -> 66 us
  other arithmetic: 60.3 us -> 23.2 us
  local copies, waits for them, and re-layouts: 54.3 us -> 37.8 us
    reduce_scatter x6 -> x5, waiting for transfers between devices: 452 us -> 245 us  [the longest x1 110 us: shards(): scatter_all(down_part.astype(low).reshape(mp * D, -1)).astype(full)]
    dot_general x40 -> x19, matrix products: 186 us -> 94.4 us  [the longest x12 52.9 us: dot_of(): lax.dot_general(left_side, right_side, (((left_dim,), (right_dim,)), ((),...]
    all_gather x5 -> x4, waiting for transfers between devices: 196 us -> 122 us  [the longest x1 57.5 us: shards(): down_weight = gather_all(w_down.T).reshape(mp, D, -1)]
    pallas_call x0 -> x2, Pallas kernels: none -> 66 us  [the longest x1 37.8 us: attend_backward(): pl.pallas_call(backward_kernel, out_shape=(jax.ShapeDtypeStruct((rows, D)...]
    all_gather x1, waiting for transfers between devices: 39 us -> 62.7 us  [shards(): first_all = lax.all_gather(first_norm, 'mp', axis=0, tiled=True)]
    convert_element_type x9 -> x5, other arithmetic: 24 us -> 5.8 us  [the longest x1 1.64 us: shards(): lax.psum_scatter(qkv_grad, 'dp', scatter_dimension=1, tiled=True)]
    reduce_sum x14 -> x8, other arithmetic: 26.5 us -> 8.98 us  [the longest x1 3.22 us: shards(): sequence_sum = jnp.sum(input_grad, axis=0)]
    unnamed x17 -> x14, waiting for transfers between devices: 72.2 us -> 63.9 us
  transfers between devices with their start and end apart: 15 -> 12, of which waited for: 13 -> 9; matrix products, arithmetic and copies ran while one was open for 7% -> 15% of each run, Pallas kernels for 0% -> 8%
where the time goes in v1:
time: 813 us; the launch traced here: 807 us
  waiting for transfers between devices  494 us (61%)
  matrix products  94.4 us (12%)
  blocking collectives  73.8 us (9%)
  Pallas kernels  66 us (8%)
  local copies, waits for them, and re-layouts  37.8 us (5%)
  other arithmetic  23.2 us (3%)
  between operations  17.6 us (2%)
    reduce_scatter x1, waiting for transfers between devices, shards(): scatter_all(down_part.astype(low).reshape(mp * D, -1)).astype(full)  110 us
    unnamed x14, waiting for transfers between devices  63.9 us
    reduce_scatter x1, waiting for transfers between devices, shards(): up_grad = scatter_all(up_part.astype(low).reshape(mp * D, -1)).astype(full)  62.7 us
    all_gather x1, waiting for transfers between devices, shards(): first_all = lax.all_gather(first_norm, 'mp', axis=0, tiled=True)  62.7 us
    all_gather x1, waiting for transfers between devices, shards(): down_weight = gather_all(w_down.T).reshape(mp, D, -1)  57.5 us
    dot_general x12, matrix products, dot_of(): lax.dot_general(left_side, right_side, (((left_dim,), (right_dim,)), ((),...  52.9 us
    all_gather x1, waiting for transfers between devices, shards(): up_weight = gather_all(w_up).reshape(mp, D, -1)  50.9 us
    psum x1, blocking collectives, shards(): total = lax.psum(packed, both)  41.2 us
  transfers between devices with their start and end apart: 12, of which 9 were waited for; matrix products, arithmetic and copies ran while one was open for 15% of the time, Pallas kernels for 8%

profile of v1, /device:TPU:0, one launch (start us, length us, event | category | flops | bytes accessed | tf_op | source)
XLA Modules:
  0.0 807.3 jit_solution(6381265451280667068)
XLA Ops:
  8.4 21.3 %all_gather.21 = bf16[3,96,768]{1,0,2:T(4,128)(2,1)S(1)} all-gather(bf16[3,96,192]{1,0,2:T(4,128)(2,1)S(1)} %copy.49), channel_id=1, replica_groups=mesh['dp'=8,'mp'=4] {'mp'}, dimensions={2}, use_global_device_ids=true | all-gather | bytes 552960 | tf_op jit(solution)/shard_map/all_gather | solution.py:214
  36.4 11.3 %all_gather.24 = bf16[192,768]{0,1:T(8,128)(2,1)S(1)} all-gather(bf16[192,96]{0,1:T(8,128)(2,1)S(1)} %copy.51), channel_id=1, replica_groups=mesh['dp'=8,'mp'=4] {'dp'}, dimensions={1}, use_global_device_ids=true | all-gather | bytes 331776 | tf_op jit(solution)/shard_map/all_gather | solution.py:218
  52.5 13.2 %all-gather.6.cloned.1.call-done = bf16[3,768,768]{2,1,0:T(8,128)(2,1)} async-done(((bf16[3,96,768]{2,1,0:T(8,128)(2,1)}), bf16[3,768,768]{2,1,0:T(8,128)(2,1)}) %all-gather.6.cloned.1.call-update) | async-done | bytes 3538960 | tf_op jit(solution)/shard_map/all_gather | solution.py:215
  68.6 62.7 %all-gather.8.cloned.1.call-done = bf16[2048,768]{1,0:T(8,128)(2,1)} async-done(((bf16[512,768]{1,0:T(8,128)(2,1)}), bf16[2048,768]{1,0:T(8,128)(2,1)}) %all-gather.8.cloned.1.call-update) | async-done | bytes 3145744 | tf_op jit(solution)/shard_map/all_gather | solution.py:223
  131.3 6.6 convolution_convert_fusion.k_ref
  137.9 5.5 add_convert_fusion.1.v_ref
  143.5 28.2 %attend_forward.1 = (f32[512,768]{1,0:T(8,128)}, f32[512,768]{1,0:T(8,128)}) custom-call(s32[1]{0:T(128)} %dynamic_slice.11.length_ref, bf16[512,768]{1,0:T(8,128)(2,1)} %fusion.19.q_ref, bf16[2048,768]{1,0:T(8,128)(2,1)} %convolution_convert_fusion.k_ref, bf16[2048,768]{1,0:T(8,128)(2,1)} %add_convert_fusion.1.v_ref), custom_call_target="tpu_custom_call" | custom-call | flops 12884901888 | bytes 18874368 | tf_op jit(solution)/shard_map/attend_forward/pallas_call | solution.py:88
  177.2 50.9 %all-gather.12.cloned.1.call-done = bf16[3072,768]{1,0:T(8,128)(2,1)} async-done(((bf16[96,768]{1,0:T(8,128)(2,1)}), bf16[3072,768]{1,0:T(8,128)(2,1)}) %all-gather.12.cloned.1.call-update) | async-done | bytes 4718608 | tf_op jit(solution)/shard_map/all_gather | solution.py:216
  228.1 7.7 fusion.9
  235.9 57.5 %all-gather.14.cloned.1.call-done = bf16[3072,768]{1,0:T(8,128)(2,1)} async-done(((bf16[96,768]{1,0:T(8,128)(2,1)}), bf16[3072,768]{1,0:T(8,128)(2,1)}) %all-gather.14.cloned.1.call-update) | async-done | bytes 4718608 | tf_op jit(solution)/shard_map/all_gather | solution.py:217
  293.4 7.5 fusion.37
  301.0 5.6 convert_reduce_fusion
  323.1 37.8 %attend_backward.1 = (bf16[512,768]{1,0:T(8,128)(2,1)}, bf16[2048,768]{1,0:T(8,128)(2,1)}, bf16[2048,768]{1,0:T(8,128)(2,1)}) custom-call(s32[1]{0:T(128)} %dynamic_slice.11.length_ref, bf16[512,768]{1,0:T(8,128)(2,1)} %fusion.19.q_ref, bf16[2048,768]{1,0:T(8,128)(2,1)} %convolution_convert_fusion.k_ref, bf16[2048,768]{1,0:T(8,128)(2,1)} %add_convert_fusion.1.v_ref, ...), custom_call_target="tpu_custom_call" | custom-call | flops 32212254720 | bytes 25165824 | tf_op jit(solution)/shard_map/attend_backward/pallas_call | solution.py:153
  360.8 7.5 fusion.20
  370.4 8.4 %add_convert_fusion = bf16[2048,768]{1,0:T(8,128)(2,1)} fusion(f32[2048,768]{1,0:T(8,128)} %fusion.20, bf16[2048,768]{1,0:T(8,128)(2,1)} %get-tuple-element.22, bf16[3,768,768]{2,1,0:T(8,128)(2,1)} %all-gather.6.cloned.1.call-done), kind=kOutput, calls=%fused_computation.15 | convolution fusion | flops 2419064832 | bytes 13762560 | tf_op jit(solution)/shard_map/dot_general | solution.py:46
  390.8 8.1 %copy.61 = bf16[3,768,768]{1,0,2:T(4,128)(2,1)} copy(bf16[3,768,768]{2,1,0:T(8,128)(2,1)} %pad_maximum_fusion) | data formatting | bytes 7077888
  403.9 7.3 convolution_convert_fusion.2
  411.5 7.3 convolution_convert_fusion.1
  427.1 38.6 %reduce-scatter.12.cloned.1.call-done = bf16[512,768]{1,0:T(8,128)(2,1)} async-done(((bf16[2048,768]{1,0:T(8,128)(2,1)}), bf16[512,768]{1,0:T(8,128)(2,1)}) %reduce-scatter.12.cloned.1.call-update) | async-done | bytes 786448 | tf_op jit(solution)/shard_map/reduce_scatter | solution.py:288
  471.8 62.7 %reduce-scatter.22.cloned.1.call-done = bf16[192,2304]{1,0:T(8,128)(2,1)} async-done(((bf16[768,2304]{1,0:T(8,128)(2,1)}), bf16[192,2304]{1,0:T(8,128)(2,1)}) %reduce-scatter.22.cloned.1.call-update) | async-done | bytes 884752
  542.4 41.2 %psum.7 = f32[20,768]{1,0:T(8,128)S(1)} all-reduce(f32[20,768]{1,0:T(8,128)S(1)} %concatenate.3), channel_id=1, replica_groups=mesh['dp'=8,'mp'=4] {'dp','mp'}, use_global_device_ids=true, to_apply=%region_21.22 | all-reduce | flops 15360 | bytes 122880 | tf_op jit(solution)/shard_map/psum | solution.py:321
  584.3 62.7 %reduce-scatter.18.cloned.1.call-done = bf16[96,768]{1,0:T(8,128)(2,1)} async-done(((bf16[3072,768]{1,0:T(8,128)(2,1)}), bf16[96,768]{1,0:T(8,128)(2,1)}) %reduce-scatter.18.cloned.1.call-update) | async-done | bytes 147472 | tf_op jit(solution)/shard_map/reduce_scatter | solution.py:276
  649.9 109.7 %reduce-scatter.20.cloned.1.call-done = bf16[96,768]{1,0:T(8,128)(2,1)} async-done(((bf16[3072,768]{1,0:T(8,128)(2,1)}), bf16[96,768]{1,0:T(8,128)(2,1)}) %reduce-scatter.20.cloned.1.call-update) | async-done | bytes 147472 | tf_op jit(solution)/shard_map/reduce_scatter | solution.py:275
  764.2 34.4 %reduce-scatter.14.cloned.1.call-done = bf16[3,96,192]{2,1,0:T(8,128)(2,1)} async-done(((bf16[3,768,192]{2,1,0:T(8,128)(2,1)}), bf16[3,96,192]{2,1,0:T(8,128)(2,1)}) %reduce-scatter.14.cloned.1.call-update) | async-done | bytes 110608 | tf_op jit(solution)/shard_map/reduce_scatter | solution.py:302
  (166 shorter events, 85.8 us)
Async XLA Ops:
  7.2 23.8 %copy-start.21 = (s32[8]{0:T(128)S(1)}, s32[8]{0:T(128)}, u32[]{:S(2)}) copy-start(s32[8]{0:T(128)} %param.17) | copy-start | bytes 100
  7.2 27.0 %copy-start.18 = (f32[2,768]{1,0:T(2,128)S(1)}, f32[2,768]{1,0:T(2,128)}, u32[]{:S(2)}) copy-start(f32[2,768]{1,0:T(2,128)} %param.20) | copy-start | bytes 18436
  7.2 27.1 %copy-start.19 = (f32[2,768]{1,0:T(2,128)S(1)}, f32[2,768]{1,0:T(2,128)}, u32[]{:S(2)}) copy-start(f32[2,768]{1,0:T(2,128)} %param.21) | copy-start | bytes 18436
  7.2 27.1 %copy-start = (bf16[512,768]{1,0:T(8,128)(2,1)S(1)}, bf16[512,768]{1,0:T(8,128)(2,1)}, u32[]{:S(2)}) copy-start(bf16[512,768]{1,0:T(8,128)(2,1)} %param.16) | copy-start | bytes 2359300
  7.2 58.4 %all-gather.6.cloned.1.call-start = ((), (), s32[]{:S(2)}) async-start(), calls=%async_computation.7 | async-start | bytes 3981312 | tf_op jit(solution)/shard_map/all_gather | solution.py:215
  30.9 100.4 %all-gather.8.cloned.1.call-start = ((), (), s32[]{:S(2)}) async-start(), calls=%async_computation.8 | async-start | bytes 3932160 | tf_op jit(solution)/shard_map/all_gather | solution.py:223
  36.2 13.6 %copy-start.29 = (s32[8]{0:T(128)S(1)}, s32[8]{0:T(128)}, u32[]{:S(2)}) copy-start(s32[8]{0:T(128)} %param.18) | copy-start | bytes 100
  36.2 15.5 %copy-start.9 = (f32[3072]{0:T(1024)S(1)}, f32[3072]{0:T(1024)}, u32[]{:S(2)}) copy-start(f32[3072]{0:T(1024)} %param.27) | copy-start | bytes 36868
  36.2 16.2 %copy-start.20 = (f32[2,768]{1,0:T(2,128)S(1)}, f32[2,768]{1,0:T(2,128)}, u32[]{:S(2)}) copy-start(f32[2,768]{1,0:T(2,128)} %param.23) | copy-start | bytes 18436
  36.2 29.4 %copy-start.4 = (bf16[512,768]{1,0:T(8,128)(2,1)S(1)}, bf16[512,768]{1,0:T(8,128)(2,1)}, u32[]{:S(2)}) copy-start(bf16[512,768]{1,0:T(8,128)(2,1)} %add_convert_fusion.4) | copy-start | bytes 2359300
  36.2 138.0 %all-gather.10.cloned.1.call-start = ((), (), s32[]{:S(2)}) async-start(), calls=%async_computation.9 | async-start | bytes 1474560 | tf_op jit(solution)/shard_map/all_gather | solution.py:219
  48.6 179.6 %all-gather.12.cloned.1.call-start = ((), (), s32[]{:S(2)}) async-start(), calls=%async_computation.10 | async-start | bytes 4866048 | tf_op jit(solution)/shard_map/all_gather | solution.py:216
  49.2 244.2 %all-gather.14.cloned.1.call-start = ((), (), s32[]{:S(2)}) async-start(), calls=%async_computation.11 | async-start | bytes 4866048 | tf_op jit(solution)/shard_map/all_gather | solution.py:217
  49.7 318.6 %reduce-scatter.16.cloned.1.call-start = ((), (), s32[]{:S(2)}) async-start(), calls=%async_computation.14 | async-start | bytes 1474560 | tf_op jit(solution)/shard_map/reduce_scatter | solution.py:303
  176.9 129.7 %copy-start.1 = (f32[512,768]{1,0:T(8,128)}, f32[512,768]{1,0:T(8,128)S(1)}, u32[]{:S(2)}) copy-start(f32[512,768]{1,0:T(8,128)S(1)} %get-tuple-element.50) | copy-start | bytes 4718596
  228.1 65.2 %copy-start.28 = (f32[768]{0:T(1024)S(1)}, f32[768]{0:T(1024)}, u32[]{:S(2)}) copy-start(f32[768]{0:T(1024)} %param.29) | copy-start | bytes 9220
  293.4 13.2 %slice-start = ((s8[4718592]{0:T(1024)(128)(4,1)}), s8[4194304]{0:T(1024)(128)(4,1)S(1)}, s32[]{:S(2)}) async-start(s8[4718592]{0:T(1024)(128)(4,1)} %bitcast.132), calls=%async_computation.19 | async-start | bytes 8388608
  323.0 102.5 %reduce-scatter.24.cloned.1.call-start = ((), (), s32[]{:S(2)}) async-start(), calls=%async_computation.18 | async-start | bytes 442368
  370.3 95.4 %reduce-scatter.12.cloned.1.call-start = ((), (), s32[]{:S(2)}) async-start(), calls=%async_computation.12 | async-start | bytes 3932160 | tf_op jit(solution)/shard_map/reduce_scatter | solution.py:288
  378.8 155.7 %reduce-scatter.22.cloned.1.call-start = ((), (), s32[]{:S(2)}) async-start(), calls=%async_computation.17 | async-start | bytes 4423680
  403.8 243.2 %reduce-scatter.18.cloned.1.call-start = ((), (), s32[]{:S(2)}) async-start(), calls=%async_computation.15 | async-start | bytes 4866048 | tf_op jit(solution)/shard_map/reduce_scatter | solution.py:276
  411.2 348.4 %reduce-scatter.20.cloned.1.call-start = ((), (), s32[]{:S(2)}) async-start(), calls=%async_computation.16 | async-start | bytes 4866048 | tf_op jit(solution)/shard_map/reduce_scatter | solution.py:275
  418.8 379.8 %reduce-scatter.14.cloned.1.call-start = ((), (), s32[]{:S(2)}) async-start(), calls=%async_computation.13 | async-start | bytes 1327104 | tf_op jit(solution)/shard_map/reduce_scatter | solution.py:302
  538.9 222.3 %copy-start.22 = (s32[8]{0:T(128)S(1)}, s32[8]{0:T(128)}, u32[]{:S(2)}) copy-start(s32[8]{0:T(128)} %param.17) | copy-start | bytes 100
  (22 other events, 89.5 us)
Sparse Core Ops, SparseCore 0:
  31.0 34.5 all-gather.5
  67.8 63.4 all-gather.7
  133.5 29.0 all-gather.9
  165.3 62.7 all-gather.11
  230.9 62.4 all-gather.13
  323.1 27.9 reduce-scatter.15
  370.4 32.6 reduce-scatter.23
  405.4 60.2 reduce-scatter.11
  468.0 66.3 reduce-scatter.21
  539.8 107.2 reduce-scatter.17
  653.4 106.0 reduce-scatter.19
  762.6 35.9 reduce-scatter.13

commit v2 on v1

v2 whole, which is shorter than its diff:
```python
import functools

import jax
import jax.numpy as jnp
from jax import lax
from jax.experimental import pallas as pl
from jax.experimental.pallas import tpu as pltpu
from jax.sharding import PartitionSpec as P

D = 768
HEADS = 12
HEAD_DIM = 64
FF = 3072
MAXLEN = 2048
PAIR = 2 * HEAD_DIM
PAIRS = HEADS // 2
KEY_BLOCK = 512

far_below = -1e30
epsilon = 1e-05
score_scale = HEAD_DIM ** (-0.5)
low = jnp.bfloat16
full = jnp.float32
both = ("dp", "mp")


def norm_stats(values):
    center = values - jnp.mean(values, axis=-1, keepdims=True)
    spread = jnp.mean(center * center, axis=-1, keepdims=True)
    inverse = lax.rsqrt(spread + epsilon)
    return center * inverse, inverse


def norm_back(unit, inverse, gain_row, grad):
    scaled = grad * gain_row
    mean_scaled = jnp.mean(scaled, axis=-1, keepdims=True)
    mean_unit = jnp.mean(scaled * unit, axis=-1, keepdims=True)
    return (
        inverse * (scaled - mean_scaled - unit * mean_unit),
        jnp.sum(grad * unit, axis=0),
        jnp.sum(grad, axis=0),
    )


def dot_of(left_side, right_side, left_dim, right_dim):
    return lax.dot_general(
        left_side,
        right_side,
        (((left_dim,), (right_dim,)), ((), ())),
        preferred_element_type=full,
    )


def first_half(shape):
    return lax.broadcasted_iota(jnp.int32, shape, len(shape) - 1) < HEAD_DIM


def forward_kernel(
    first, last, scalars, q_ref, k_ref, v_ref, *refs
):
    if first:
        outs = refs
    else:
        top_in, sum_in, acc_in = refs[:3]
        outs = refs[3:]
    rows = q_ref.shape[0]
    keys = k_ref.shape[0]
    limit = scalars[1] - scalars[0] * keys
    place = lax.broadcasted_iota(jnp.int32, (1, keys), 1)
    bias = jnp.where(place < limit, 0.0, far_below)
    q_pair = q_ref[...]
    k_pair = k_ref[...]
    v_pair = v_ref[...]
    lower = first_half((rows, PAIR))
    parts = []
    for half in range(2):
        kept = lower if half == 0 else jnp.logical_not(lower)
        lane = half * HEAD_DIM
        q_half = jnp.where(kept, q_pair, jnp.zeros_like(q_pair))
        scores = dot_of(q_half, k_pair, 1, 1) + bias
        highest = jnp.max(scores, axis=-1, keepdims=True)
        if first:
            highest = jnp.maximum(highest, far_below)
            exp_scores = jnp.exp(scores - highest)
            totals = jnp.sum(exp_scores, axis=-1, keepdims=True)
            mixed = dot_of(exp_scores.astype(low), v_pair, 1, 0)
        else:
            before = top_in[:, lane : lane + 1]
            highest = jnp.maximum(highest, before)
            shrink = jnp.exp(before - highest)
            exp_scores = jnp.exp(scores - highest)
            totals = sum_in[:, lane : lane + 1] * shrink + jnp.sum(
                exp_scores, axis=-1, keepdims=True
            )
            mixed = acc_in[...] * shrink + dot_of(exp_scores.astype(low), v_pair, 1, 0)
        parts.append((highest, totals, mixed))
    top = jnp.where(lower, parts[0][0], parts[1][0])
    total = jnp.where(lower, parts[0][1], parts[1][1])
    mixed = jnp.where(lower, parts[0][2], parts[1][2])
    if last:
        out_ref, log_ref = outs
        out_ref[...] = mixed / total
        log_ref[...] = top + jnp.log(total)
    else:
        top_ref, sum_ref, acc_ref = outs
        top_ref[...] = top
        sum_ref[...] = total
        acc_ref[...] = mixed


def attend_forward(queries, keys, values, scalars, state, last):
    rows, total = queries.shape[0], keys.shape[0]
    first = state is None
    pair_rows = lambda count: pl.BlockSpec((count, PAIR), lambda i, n: (0, i))
    wide = jax.ShapeDtypeStruct((rows, D), full)
    carried = () if first else state
    return pl.pallas_call(
        functools.partial(forward_kernel, first, last),
        out_shape=(wide,) * (2 if last else 3),
        grid_spec=pltpu.PrefetchScalarGridSpec(
            num_scalar_prefetch=1,
            grid=(PAIRS,),
            in_specs=[pair_rows(rows), pair_rows(total), pair_rows(total)]
            + [pair_rows(rows)] * len(carried),
            out_specs=[pair_rows(rows)] * (2 if last else 3),
        ),
        compiler_params=pltpu.CompilerParams(vmem_limit_bytes=40 << 20),
        cost_estimate=pl.CostEstimate(
            flops=4 * rows * total * D * 4,
            bytes_accessed=12 * total * D,
            transcendentals=rows * total * HEADS,
        ),
        name="attend_forward",
    )(scalars, queries, keys, values, *carried)


def backward_kernel(
    first, last, scalars, q_ref, k_ref, v_ref, g_ref, log_ref, delta_ref, *refs
):
    if first:
        dq_ref, dk_ref, dv_ref = refs
    else:
        dq_in, dq_ref, dk_ref, dv_ref = refs
    rows = q_ref.shape[0]
    keys = k_ref.shape[0]
    limit = scalars[1] - scalars[0] * keys
    q_pair = q_ref[...]
    g_pair = g_ref[...]
    k_pair = k_ref[...]
    v_pair = v_ref[...]
    lower = first_half((rows, PAIR))
    lower_keys = first_half((keys, PAIR))
    place = lax.broadcasted_iota(jnp.int32, (keys, 1), 0)
    bias = jnp.where(place < limit, 0.0, far_below)
    dq = []
    dk = []
    dv = []
    for half in range(2):
        kept = lower if half == 0 else jnp.logical_not(lower)
        q_half = jnp.where(kept, q_pair, jnp.zeros_like(q_pair))
        g_half = jnp.where(kept, g_pair, jnp.zeros_like(g_pair))
        log_row = log_ref[0, half : half + 1, :]
        delta_row = delta_ref[0, half : half + 1, :]
        scores = dot_of(k_pair, q_half, 1, 1) + bias
        probs = jnp.exp(scores - log_row)
        dv.append(dot_of(probs.astype(low), g_pair, 1, 0))
        prob_grad = dot_of(v_pair, g_half, 1, 1)
        score_grad = (probs * (prob_grad - delta_row)).astype(low)
        dk.append(dot_of(score_grad, q_pair, 1, 0))
        dq.append(dot_of(score_grad, k_pair, 0, 0))
    dk_ref[...] = jnp.where(lower_keys, dk[0], dk[1]).astype(low)
    dv_ref[...] = jnp.where(lower_keys, dv[0], dv[1]).astype(low)
    dq_all = jnp.where(lower, dq[0], dq[1])
    if not first:
        dq_all = dq_all + dq_in[...]
    if last:
        dq_ref[...] = (dq_all * score_scale).astype(low)
    else:
        dq_ref[...] = dq_all


def attend_backward(queries, keys, values, grads, logs, deltas, scalars, carried, last):
    rows, total = queries.shape[0], keys.shape[0]
    first = carried is None
    extra = () if first else (carried,)
    pair_rows = lambda count: pl.BlockSpec((count, PAIR), lambda i, n: (0, i))
    stats = pl.BlockSpec((1, 2, rows), lambda i, n: (i, 0, 0))
    return pl.pallas_call(
        functools.partial(backward_kernel, first, last),
        out_shape=(
            jax.ShapeDtypeStruct((rows, D), low if last else full),
            jax.ShapeDtypeStruct((total, D), low),
            jax.ShapeDtypeStruct((total, D), low),
        ),
        grid_spec=pltpu.PrefetchScalarGridSpec(
            num_scalar_prefetch=1,
            grid=(PAIRS,),
            in_specs=[
                pair_rows(rows),
                pair_rows(total),
                pair_rows(total),
                pair_rows(rows),
                stats,
                stats,
            ]
            + [pair_rows(rows)] * len(extra),
            out_specs=[pair_rows(rows), pair_rows(total), pair_rows(total)],
        ),
        compiler_params=pltpu.CompilerParams(vmem_limit_bytes=40 << 20),
        cost_estimate=pl.CostEstimate(
            flops=10 * rows * total * D * 4,
            bytes_accessed=16 * total * D,
            transcendentals=rows * total * HEADS,
        ),
        name="attend_backward",
    )(scalars, queries, keys, values, grads, logs, deltas, *extra)


def swap(value, axis, bit):
    count = lax.axis_size(axis)
    return lax.ppermute(value, axis, [(i, i ^ bit) for i in range(count)])


def outer_bits():
    bits = []
    bit = 2
    while bit < lax.axis_size("dp"):
        bits.append(bit)
        bit *= 2
    return bits


def gather_dp(parts):
    bits = outer_bits()
    half = len(bits) // 2
    orders = [bits[half * (n % 2) :] + bits[: half * (n % 2)] for n in range(len(parts))]
    held = [[([0], part)] for part in parts]
    for step in range(len(bits)):
        arrived = []
        for n in range(len(parts)):
            bit = orders[n][step]
            masks = [m for mask, _ in held[n] for m in mask]
            block = jnp.concatenate([array for _, array in held[n]]) if len(held[n]) > 1 else held[n][0][1]
            arrived.append([(masks, block), ([m ^ bit for m in masks], swap(block, "dp", bit))])
        held = arrived
    return [
        pieces + [([m ^ 1 for m in masks], swap(block, "dp", 1)) for masks, block in pieces]
        for pieces in held
    ]


def place_kernel(plan, *refs):
    count = len(plan)
    ins = refs[:count]
    outs = refs[count:-1]
    sems = refs[-1]
    me = lax.axis_index("dp")
    rank = lax.axis_index("mp")
    copies = []
    for ref, moves in zip(ins, plan):
        for start, size, which, mask, rank_mask, stride, offset in moves:
            row = (me ^ mask) * 96 + offset
            if stride:
                row = row + (rank ^ rank_mask) * stride
            copy = pltpu.make_async_copy(
                ref.at[pl.ds(start, size), :],
                outs[which].at[pl.ds(pl.multiple_of(row, 16), size), :],
                sems.at[len(copies)],
            )
            copy.start()
            copies.append(copy)
    for copy in copies:
        copy.wait()


def place(gathered, layouts, shapes):
    arrays = []
    plan = []
    for pieces, layout in zip(gathered, layouts):
        rows = sum(size for _, size, *_ in layout)
        for masks, array in pieces:
            moves = []
            for j, mask in enumerate(masks):
                for start, size, which, rank_mask, stride, offset in layout:
                    moves.append((j * rows + start, size, which, mask, rank_mask, stride, offset))
            arrays.append(array)
            plan.append(moves)
    moved = sum(array.size for array in arrays) * 4
    return pl.pallas_call(
        functools.partial(place_kernel, plan),
        out_shape=[jax.ShapeDtypeStruct(shape, low) for shape in shapes],
        in_specs=[pl.BlockSpec(memory_space=pl.ANY)] * len(arrays),
        out_specs=[pl.BlockSpec(memory_space=pl.ANY)] * len(shapes),
        scratch_shapes=[pltpu.SemaphoreType.DMA((sum(len(moves) for moves in plan),))],
        cost_estimate=pl.CostEstimate(flops=0, bytes_accessed=moved, transcendentals=0),
        name="place",
    )(*arrays)


def scatter_dp(values):
    bits = outer_bits()
    half = len(bits) // 2
    orders = [[1] + bits[half * (n % 2) :] + bits[: half * (n % 2)] for n in range(len(values))]
    me = lax.axis_index("dp")
    held = []
    for value in values:
        lead, dp = value.shape[0], value.shape[1]
        dims = (2,) * (len(bits) + 1)
        held.append(value.reshape((lead,) + dims + value.shape[2:]))
    axes = [list(reversed([1] + bits)) for _ in values]
    for step in range(len(bits) + 1):
        sends = []
        keeps = []
        for n, value in enumerate(held):
            bit = orders[n][step]
            axis = 1 + axes[n].index(bit)
            axes[n].remove(bit)
            mine = (me // bit) % 2
            keeps.append(lax.dynamic_index_in_dim(value, mine, axis, keepdims=False))
            sends.append(lax.dynamic_index_in_dim(value, 1 - mine, axis, keepdims=False))
        got = [swap(send.astype(low), "dp", orders[n][step]) for n, send in enumerate(sends)]
        held = [keep.astype(full) + other.astype(full) for keep, other in zip(keeps, got)]
        if step < len(bits):
            held = [value.astype(low) for value in held]
    return held


def scatter_mp(value):
    rank = lax.axis_index("mp")
    for bit in (2, 1):
        mine = (rank // bit) % 2
        pair = value.reshape((2, value.shape[0] // 2) + value.shape[1:])
        keep = lax.dynamic_index_in_dim(pair, mine, 0, keepdims=False)
        send = lax.dynamic_index_in_dim(pair, 1 - mine, 0, keepdims=False)
        value = keep.astype(full) + swap(send.astype(low), "mp", bit).astype(full)
    return value[0]


def shards(
    tokens_in,
    timesteps,
    lengths,
    time_table,
    norm_gains,
    norm_biases,
    w_qkv,
    qv_bias,
    w_out,
    out_bias,
    w_up,
    up_bias,
    w_down,
    down_bias,
    cotangent,
    teacher,
):
    rank = lax.axis_index("mp")
    data_rank = lax.axis_index("dp")
    mp = lax.axis_size("mp")
    dp = lax.axis_size("dp")
    own_rows = tokens_in.shape[0]
    length = lax.dynamic_index_in_dim(lengths, data_rank, keepdims=False)
    own_time = lax.dynamic_index_in_dim(timesteps, data_rank, keepdims=False)
    position = rank * own_rows + jnp.arange(own_rows)
    row_valid = position < length
    odd = rank % 2 == 1
    upper = rank >= 2
    middle = jnp.logical_or(rank == 1, rank == 2)

    block = w_qkv.shape[1]
    narrow = jnp.concatenate([w_qkv.reshape(3 * block, -1), w_out.T])
    other = swap(narrow, "mp", 1)
    pair = jnp.concatenate(
        [jnp.where(odd, other, narrow), jnp.where(odd, narrow, other)], axis=1
    )
    other = swap(pair, "mp", 2)
    wide = jnp.concatenate(
        [jnp.where(upper, other, pair), jnp.where(upper, pair, other)], axis=1
    )
    qkv_rows, out_rows = wide[: 3 * block], wide[3 * block :]
    aligned = block % 32 == 0
    if aligned:
        split = 3 * block // 2
        gathered = gather_dp([qkv_rows[:split], qkv_rows[split:]])
        (qkv_weight,) = place(
            gathered,
            [
                [(0, block, 0, 0, 0, 0), (block, split - block, 0, 0, 0, D)],
                [
                    (0, 2 * block - split, 0, 0, 0, D + split - block),
                    (2 * block - split, block, 0, 0, 0, 2 * D),
                ],
            ],
            [(3 * D, D)],
        )
        qkv_weight = qkv_weight.reshape(3, D, D)
    else:
        qkv_weight = lax.all_gather(
            qkv_rows.reshape(3, block, D), "dp", axis=1, tiled=True
        )

    table_row = lax.dynamic_slice_in_dim(time_table, own_time, 1)
    start_state = tokens_in.astype(full) + table_row.astype(full)
    unit_one, inverse_one = norm_stats(start_state)
    first_norm = (unit_one * norm_gains[0] + norm_biases[0]).astype(low)
    rightward = lambda value, pairs: lax.ppermute(value, "mp", pairs)
    from_left = rightward(first_norm, [(0, 1), (1, 2), (2, 3)])
    from_right = rightward(first_norm, [(1, 0), (2, 1), (3, 2)])
    near = jnp.where(rank == 0, from_right, from_left)
    second = jnp.where(
        upper,
        rightward(from_left, [(1, 2), (2, 3)]),
        rightward(from_right, [(1, 0), (2, 1)]),
    )
    last = jnp.where(middle, from_right, rightward(second, [(1, 0), (2, 3)]))
    chunks = [first_norm, near, second, last]
    indices = [
        rank,
        jnp.where(rank == 0, 1, rank - 1),
        jnp.where(upper, rank - 2, rank + 2),
        jnp.where(middle, rank + 1, 3 - rank),
    ]
    scalars = [jnp.stack([index, length]).astype(jnp.int32) for index in indices]

    if aligned:
        tall = jnp.concatenate([w_up, w_down.T])
        pair = jnp.concatenate([tall, swap(tall, "mp", 1)])
        other = swap(pair, "mp", 2)
        parts = [
            jnp.concatenate([pair, out_rows[: block // 2]]),
            jnp.concatenate([other, out_rows[block // 2 :]]),
        ]
        gathered = gather_dp(parts)
        layout = lambda masks, shift: [
            (0, block, 0, masks[0], D, 0),
            (block, block, 1, masks[0], D, 0),
            (2 * block, block, 0, masks[1], D, 0),
            (3 * block, block, 1, masks[1], D, 0),
            (4 * block, block // 2, 2, 0, 0, shift),
        ]
        up_weight, down_weight, out_weight = place(
            gathered,
            [layout((0, 1), 0), layout((2, 3), block // 2)],
            [(mp * D, D), (mp * D, D), (D, D)],
        )
    else:
        out_weight = lax.all_gather(out_rows, "dp", axis=0, tiled=True)
        up_weight = lax.all_gather(w_up, ("mp", "dp"), axis=0, tiled=True)
        down_weight = lax.all_gather(w_down.T, ("mp", "dp"), axis=0, tiled=True)
    up_weight = up_weight.reshape(mp, D, D)
    down_weight = down_weight.reshape(mp, D, D)

    queries = dot_of(first_norm, qkv_weight[0], 1, 0) + qv_bias[0]
    queries = (queries.astype(low) * score_scale).astype(low)
    keys = []
    values = []
    state = None
    for n, chunk in enumerate(chunks):
        keys.append(dot_of(chunk, qkv_weight[1], 1, 0).astype(low))
        values.append((dot_of(chunk, qkv_weight[2], 1, 0) + qv_bias[1]).astype(low))
        state = attend_forward(queries, keys[n], values[n], scalars[n], state, n == 3)
    mixed, logs = state
    attended = mixed.astype(low)

    middle_state = start_state + dot_of(attended, out_weight, 1, 1) + out_bias
    unit_two, inverse_two = norm_stats(middle_state)
    second_norm = (unit_two * norm_gains[1] + norm_biases[1]).astype(low)
    hidden_pre = jnp.einsum(
        "td,mdf->mtf", second_norm, up_weight, preferred_element_type=full
    ) + up_bias.reshape(mp, 1, -1)
    error = lax.erf(hidden_pre * (0.5**0.5))
    cumulative = 0.5 * (1.0 + error)
    hidden_act = (hidden_pre * cumulative).astype(low)
    act_slope = cumulative + hidden_pre * jnp.exp(-0.5 * hidden_pre * hidden_pre) * (
        (2.0 * jnp.pi) ** -0.5
    )
    final_state = (
        middle_state
        + jnp.einsum("mtf,mdf->td", hidden_act, down_weight, preferred_element_type=full)
        + down_bias
    )
    output = final_state.astype(low)
    loss_weight = lengths.shape[0] * MAXLEN / jnp.sum(lengths).astype(full)
    final_grad = jnp.where(
        row_valid[:, None],
        cotangent.astype(full) + loss_weight * (final_state - teacher.astype(full)),
        0.0,
    )
    final_low = final_grad.astype(low)
    down_part = jnp.einsum("td,mtf->mdf", final_low, hidden_act, preferred_element_type=full)
    act_grad = jnp.einsum("td,mdf->mtf", final_low, down_weight, preferred_element_type=full)
    pre_grad = (act_slope * act_grad).astype(low)
    up_part = jnp.einsum("td,mtf->mdf", second_norm, pre_grad, preferred_element_type=full)
    up_bias_part = jnp.sum(pre_grad, axis=1, dtype=full).reshape(FF)
    second_grad = jnp.einsum("mtf,mdf->td", pre_grad, up_weight, preferred_element_type=full)
    middle_part, gain_two, shift_two = norm_back(
        unit_two, inverse_two, norm_gains[1], second_grad
    )
    middle_grad = final_grad + middle_part
    middle_low = middle_grad.astype(low)
    out_part = dot_of(middle_low, attended, 0, 0)
    attended_grad = dot_of(middle_low, out_weight, 1, 0).astype(low)

    deltas = jnp.sum(
        (attended_grad.astype(full) * mixed).reshape(own_rows, HEADS, HEAD_DIM), axis=-1
    )
    deltas = deltas.T.reshape(PAIRS, 2, own_rows)
    logs = logs.reshape(own_rows, HEADS, HEAD_DIM)[:, :, 0].T.reshape(PAIRS, 2, own_rows)
    key_grads = [None] * 4
    value_grads = [None] * 4
    firsts = [None] * 4
    query_grad = None
    sent_last = sent_right = sent_left = None
    for n in (3, 2, 1, 0):
        query_grad, key_grads[n], value_grads[n] = attend_backward(
            queries,
            keys[n],
            values[n],
            attended_grad,
            logs,
            deltas,
            scalars[n],
            query_grad,
            n == 0,
        )
        firsts[n] = dot_of(key_grads[n], qkv_weight[1], 1, 1) + dot_of(
            value_grads[n], qkv_weight[2], 1, 1
        )
        if n == 3:
            back_last = rightward(firsts[3].astype(low), [(0, 1), (3, 2)]).astype(full)
        elif n == 2:
            payload = (firsts[2] + back_last).astype(low)
            back_right = rightward(payload, [(0, 1), (1, 2)]).astype(full)
            back_left = rightward(payload, [(3, 2), (2, 1)]).astype(full)
        elif n == 1:
            to_right = jnp.where(rank == 0, firsts[1], firsts[3] + back_right).astype(low)
            to_left = (firsts[1] + back_left).astype(low)
            final_right = rightward(to_right, [(0, 1), (1, 2), (2, 3)])
            final_left = rightward(to_left, [(3, 2), (2, 1), (1, 0)])
    first_grad = (
        firsts[0]
        + dot_of(query_grad, qkv_weight[0], 1, 1)
        + final_right.astype(full)
        + final_left.astype(full)
    )
    chunk_all = jnp.concatenate(chunks)
    qkv_part = jnp.stack(
        [
            dot_of(first_norm, query_grad, 0, 0).astype(low),
            dot_of(chunk_all, jnp.concatenate(key_grads), 0, 0).astype(low),
            dot_of(chunk_all, jnp.concatenate(value_grads), 0, 0).astype(low),
        ]
    ).reshape(3, dp, block, D)
    qv_bias_part = jnp.stack(
        [
            jnp.sum(query_grad, axis=0, dtype=full),
            sum(jnp.sum(grad, axis=0, dtype=full) for grad in value_grads),
        ]
    )

    up_own, down_own = scatter_dp(
        [
            jnp.concatenate([up_part.astype(low).reshape(mp, dp, block, D), out_part.astype(low).reshape(1, dp, block, D)]),
            down_part.astype(low).reshape(mp, dp, block, D),
        ]
    )
    out_own = up_own[mp].reshape(block, mp, -1).transpose(1, 0, 2)
    tall = scatter_mp(jnp.concatenate([up_own[:mp], down_own], axis=1))
    up_grad = tall[:block]
    down_grad = tall[block:].T
    out_grad = scatter_mp(out_own).T
    left_part, right_part = scatter_dp([qkv_part[..., : D // 2], qkv_part[..., D // 2 :]])
    keep = jnp.where(upper, right_part, left_part)
    keep = keep + swap(jnp.where(upper, left_part, right_part).astype(low), "mp", 2).astype(full)
    width = D // mp
    here = jnp.where(odd, keep[..., width:], keep[..., :width])
    there = jnp.where(odd, keep[..., :width], keep[..., width:])
    qkv_grad = here + swap(there.astype(low), "mp", 1).astype(full)

    start_part, gain_one, shift_one = norm_back(
        unit_one, inverse_one, norm_gains[0], first_grad
    )
    input_grad = middle_grad + start_part
    sequence_sum = jnp.sum(input_grad, axis=0)
    own_slot = (jnp.arange(dp) == data_rank).astype(full)
    total = jnp.concatenate(
        [
            jnp.stack([gain_one, gain_two, shift_one, shift_two]),
            qv_bias_part,
            jnp.stack([jnp.sum(middle_grad, axis=0), jnp.sum(final_grad, axis=0)]),
            up_bias_part.reshape(-1, D),
            own_slot[:, None] * sequence_sum[None, :],
        ]
    )
    for bit in [1] + outer_bits():
        total = total + swap(total, "dp", bit)
    for bit in (1, 2):
        total = total + swap(total, "mp", bit)
    fixed = 8 + FF // D
    chosen = (timesteps[None, :] == jnp.arange(time_table.shape[0])[:, None]).astype(full)
    table_grad = lax.dot_general(
        chosen,
        total[fixed:],
        (((1,), (0,)), ((), ())),
        precision=lax.Precision.HIGHEST,
        preferred_element_type=full,
    )
    return (
        output,
        input_grad,
        table_grad,
        total[0:2],
        total[2:4],
        qkv_grad,
        total[4:6],
        out_grad,
        total[6],
        up_grad,
        total[8:fixed].reshape(FF),
        down_grad,
        total[7],
    )


def solution(mesh):
    rows = P(both, None)
    placed = (
        rows,
        P(),
        P(),
        P(),
        P(),
        P(),
        P(None, "dp", "mp"),
        P(),
        P("mp", "dp"),
        P(),
        P("dp", "mp"),
        P(),
        P("mp", "dp"),
        P(),
        rows,
        rows,
    )
    return jax.shard_map(
        shards,
        mesh=mesh,
        in_specs=placed,
        out_specs=(
            rows,
            rows,
            P(),
            P(),
            P(),
            P(None, "dp", "mp"),
            P(),
            P("mp", "dp"),
            P(),
            P("dp", "mp"),
            P(),
            P("mp", "dp"),
            P(),
        ),
        check_vma=False,
    )
```

time: 813 us -> 927 us (1.14)
  Pallas kernels: 66 us -> 549 us
  waiting for transfers between devices: 494 us -> 175 us
  starting transfers between devices: 0.88 us -> 78.7 us
  blocking collectives: 73.8 us -> 0 us
  matrix products: 94.4 us -> 57.8 us
  local copies, waits for them, and re-layouts: 37.8 us -> 25.6 us
  between operations: 17.6 us -> 5.68 us
    pallas_call x2 -> x10, Pallas kernels: 66 us -> 549 us  [the longest x2 432 us: place(): pl.pallas_call(functools.partial(place_kernel, plan), out_shape=[jax.Shap...]
    reduce_scatter x5 -> x0, waiting for transfers between devices: 245 us -> none  [the longest x1 110 us: shards(): scatter_all(down_part.astype(low).reshape(mp * D, -1)).astype(full)]
    all_gather x5 -> x0, waiting for transfers between devices: 184 us -> none  [the longest x1 62.7 us: shards(): first_all = lax.all_gather(first_norm, 'mp', axis=0, tiled=True)]
    ppermute x0 -> x53, waiting for transfers between devices: none -> 175 us  [the longest x43 119 us: swap(): return lax.ppermute(value, axis, [(i, i ^ bit) for i in range(count)])]
    ppermute x0 -> x53, starting transfers between devices: none -> 78.7 us  [the longest x43 45.4 us: swap(): return lax.ppermute(value, axis, [(i, i ^ bit) for i in range(count)])]
    unnamed x14 -> x0, waiting for transfers between devices: 63.9 us -> none
    psum x1 -> x0, blocking collectives: 41.2 us -> none  [shards(): total = lax.psum(packed, both)]
    all_gather x2 -> x0, blocking collectives: 32.6 us -> none  [the longest x1 21.3 us: shards(): qkv_weight = lax.all_gather(w_qkv, 'mp', axis=2, tiled=True)]
  transfers between devices with their start and end apart: 12 -> 53, of which waited for: 9 -> 19; matrix products, arithmetic and copies ran while one was open for 15% -> 6% of each run, Pallas kernels for 8% -> 20%
where the time goes in v2:
time: 927 us; the launch traced here: 921 us
  Pallas kernels  549 us (59%)
  waiting for transfers between devices  175 us (19%)
  starting transfers between devices  78.7 us (8%)
  matrix products  57.8 us (6%)
  other arithmetic  28.7 us (3%)
  local copies, waits for them, and re-layouts  25.6 us (3%)
    pallas_call x2, Pallas kernels, place(): pl.pallas_call(functools.partial(place_kernel, plan), out_shape=[jax.Shap...  432 us
    ppermute x43, waiting for transfers between devices, swap(): return lax.ppermute(value, axis, [(i, i ^ bit) for i in range(count)])  119 us
    pallas_call x4, Pallas kernels, attend_forward(): pl.pallas_call(functools.partial(forward_kernel, first, last), out_shape=...  71.7 us
    ppermute x10, waiting for transfers between devices, shards(): rightward = lambda value, pairs: lax.ppermute(value, 'mp', pairs)  56 us
    ppermute x43, starting transfers between devices, swap(): return lax.ppermute(value, axis, [(i, i ^ bit) for i in range(count)])  45.4 us
    pallas_call x4, Pallas kernels, attend_backward(): pl.pallas_call(functools.partial(backward_kernel, first, last), out_shape...  44.8 us
    ppermute x10, starting transfers between devices, shards(): rightward = lambda value, pairs: lax.ppermute(value, 'mp', pairs)  33.3 us
    dot_general x24, matrix products, dot_of(): lax.dot_general(left_side, right_side, (((left_dim,), (right_dim,)), ((),...  31.2 us
  transfers between devices with their start and end apart: 53, of which 19 were waited for; matrix products, arithmetic and copies ran while one was open for 6% of the time, Pallas kernels for 20%

profile of v2, /device:TPU:0, one launch (start us, length us, event | category | flops | bytes accessed | tf_op | source)
XLA Modules:
  0.0 920.6 jit_solution(13177589204647216305)
XLA Ops:
  24.1 23.2 %collective-permute-done.1 = bf16[384,384]{1,0:T(8,128)(2,1)S(1)} collective-permute-done((bf16[384,384]{1,0:T(8,128)(2,1)}, bf16[384,384]{1,0:T(8,128)(2,1)S(1)}, u32[]{:S(2)}, u32[]{:S(2)}) %collective-permute-start.1) | collective-permute-done | bytes 294944 | tf_op jit(solution)/shard_map/ppermute | solution.py:221
  51.9 7.8 collective-permute-done.20
  67.5 18.4 %collective-permute-done.3.refs_1_ = bf16[288,768]{1,0:T(8,128)(2,1)S(1)} collective-permute-done((bf16[288,768]{1,0:T(8,128)(2,1)S(1)}, bf16[288,768]{1,0:T(8,128)(2,1)S(1)}, u32[]{:S(2)}, u32[]{:S(2)}) %collective-permute-start.3) | collective-permute-done | bytes 442400 | tf_op jit(solution)/shard_map/ppermute | solution.py:221
  97.8 108.6 %place.2 = bf16[2304,768]{1,0:T(8,128)(2,1)} custom-call(bf16[288,768]{1,0:T(8,128)(2,1)} %copy-done.31, bf16[288,768]{1,0:T(8,128)(2,1)} %copy-done.47, bf16[288,768]{1,0:T(8,128)(2,1)} %collective-permute-done.4.refs_2_, bf16[288,768]{1,0:T(8,128)(2,1)} %collective-permute-done.5.refs_3_, bf16[288,768]{1,0:T(8,128)(2,1)} %copy-done.32, ...), custom_call_target="tpu_custom_call" | custom-call | bytes 7077888 | tf_op jit(solution)/shard_map/place/pallas_call | solution.py:289
  212.3 8.1 attend_forward.4
  222.1 19.9 %collective-permute-done.14 = bf16[512,768]{1,0:T(8,128)(2,1)S(1)} collective-permute-done((bf16[512,768]{1,0:T(8,128)(2,1)S(1)}, bf16[512,768]{1,0:T(8,128)(2,1)S(1)}, u32[]{:S(2)}, u32[]{:S(2)}) %collective-permute-start.14) | collective-permute-done | bytes 786464 | tf_op jit(solution)/shard_map/ppermute | solution.py:406
  247.1 21.1 %attend_forward.5 = (f32[512,768]{1,0:T(8,128)S(1)}, f32[512,768]{1,0:T(8,128)S(1)}, f32[512,768]{1,0:T(8,128)S(1)}) custom-call(s32[2]{0:T(128)S(1)} %get-tuple-element.124.scalars, bf16[512,768]{1,0:T(8,128)(2,1)S(1)} %fusion.48.q_ref, bf16[512,768]{1,0:T(8,128)(2,1)S(1)} %convolution_convert_fusion.6.k_ref, bf16[512,768]{1,0:T(8,128)(2,1)S(1)} %add_convert_fusion.4.v_ref, ...), custom_call_target="tpu_custom_call" | custom-call | flops 3221225472 | bytes 4718592 | tf_op jit(solution)/shard_map/attend_forward/pallas_call | solution.py:117
  268.2 21.1 %attend_forward.6 = (f32[512,768]{1,0:T(8,128)S(1)}, f32[512,768]{1,0:T(8,128)S(1)}, f32[512,768]{1,0:T(8,128)S(1)}) custom-call(s32[2]{0:T(128)S(1)} %pad_add_fusion.1.scalars, bf16[512,768]{1,0:T(8,128)(2,1)S(1)} %fusion.48.q_ref, bf16[512,768]{1,0:T(8,128)(2,1)S(1)} %convolution_convert_fusion.7.k_ref, bf16[512,768]{1,0:T(8,128)(2,1)S(1)} %add_convert_fusion.5.v_ref, ...), custom_call_target="tpu_custom_call" | custom-call | flops 3221225472 | bytes 4718592 | tf_op jit(solution)/shard_map/attend_forward/pallas_call | solution.py:117
  289.4 21.4 %attend_forward.7 = (f32[512,768]{1,0:T(8,128)S(1)}, f32[512,768]{1,0:T(8,128)S(1)}) custom-call(s32[2]{0:T(128)S(1)} %get-tuple-element.123.scalars, bf16[512,768]{1,0:T(8,128)(2,1)S(1)} %fusion.48.q_ref, bf16[512,768]{1,0:T(8,128)(2,1)S(1)} %convolution_convert_fusion.8.k_ref, bf16[512,768]{1,0:T(8,128)(2,1)S(1)} %add_convert_fusion.6.v_ref, ...), custom_call_target="tpu_custom_call" | custom-call | flops 3221225472 | bytes 4718592 | tf_op jit(solution)/shard_map/attend_forward/pallas_call | solution.py:117
  313.5 323.5 %place.3 = (bf16[3072,768]{1,0:T(8,128)(2,1)}, bf16[3072,768]{1,0:T(8,128)(2,1)}, bf16[768,768]{1,0:T(8,128)(2,1)}) custom-call(bf16[864,768]{1,0:T(8,128)(2,1)} %constant_dynamic-update-slice_fusion.refs_0_, bf16[864,768]{1,0:T(8,128)(2,1)} %collective-permute-done.17.refs_1_, bf16[864,768]{1,0:T(8,128)(2,1)} %collective-permute-done.18.refs_2_, ...), custom_call_target="tpu_custom_call" | custom-call | bytes 21233664 | tf_op jit(solution)/shard_map/place/pallas_call | solution.py:289
  675.0 11.0 %attend_backward.4 = (f32[512,768]{1,0:T(8,128)S(1)}, bf16[512,768]{1,0:T(8,128)(2,1)S(1)}, bf16[512,768]{1,0:T(8,128)(2,1)S(1)}) custom-call(s32[2]{0:T(128)S(1)} %get-tuple-element.123.scalars, bf16[512,768]{1,0:T(8,128)(2,1)S(1)} %copy-done.9, bf16[512,768]{1,0:T(8,128)(2,1)S(1)} %copy-done.7, bf16[512,768]{1,0:T(8,128)(2,1)S(1)} %copy-done.17, ...), custom_call_target="tpu_custom_call" | custom-call | flops 8053063680 | bytes 6291456 | tf_op jit(solution)/shard_map/attend_backward/pallas_call | solution.py:188
  686.1 11.2 %attend_backward.5 = (f32[512,768]{1,0:T(8,128)S(1)}, bf16[512,768]{1,0:T(8,128)(2,1)S(1)}, bf16[512,768]{1,0:T(8,128)(2,1)S(1)}) custom-call(s32[2]{0:T(128)S(1)} %pad_add_fusion.1.scalars, bf16[512,768]{1,0:T(8,128)(2,1)S(1)} %copy-done.9, bf16[512,768]{1,0:T(8,128)(2,1)S(1)} %copy-done.3, bf16[512,768]{1,0:T(8,128)(2,1)S(1)} %copy-done.13, ...), custom_call_target="tpu_custom_call" | custom-call | flops 8053063680 | bytes 6291456 | tf_op jit(solution)/shard_map/attend_backward/pallas_call | solution.py:188
  697.3 11.2 %attend_backward.6 = (f32[512,768]{1,0:T(8,128)S(1)}, bf16[512,768]{1,0:T(8,128)(2,1)S(1)}, bf16[512,768]{1,0:T(8,128)(2,1)S(1)}) custom-call(s32[2]{0:T(128)S(1)} %get-tuple-element.124.scalars, bf16[512,768]{1,0:T(8,128)(2,1)S(1)} %copy-done.9, bf16[512,768]{1,0:T(8,128)(2,1)S(1)} %copy-done.5, bf16[512,768]{1,0:T(8,128)(2,1)S(1)} %copy-done.15, ...), custom_call_target="tpu_custom_call" | custom-call | flops 8053063680 | bytes 6291456 | tf_op jit(solution)/shard_map/attend_backward/pallas_call | solution.py:188
  708.5 11.4 %attend_backward.7 = (bf16[512,768]{1,0:T(8,128)(2,1)S(1)}, bf16[512,768]{1,0:T(8,128)(2,1)S(1)}, bf16[512,768]{1,0:T(8,128)(2,1)S(1)}) custom-call(s32[2]{0:T(128)S(1)} %pad_add_fusion.3.scalars, bf16[512,768]{1,0:T(8,128)(2,1)S(1)} %copy-done.9, bf16[512,768]{1,0:T(8,128)(2,1)S(1)} %copy-done.1, bf16[512,768]{1,0:T(8,128)(2,1)S(1)} %copy-done.11, ...), custom_call_target="tpu_custom_call" | custom-call | flops 8053063680 | bytes 6291456 | tf_op jit(solution)/shard_map/attend_backward/pallas_call | solution.py:188
  734.8 9.9 %collective-permute-start.25 = (bf16[512,768]{1,0:T(8,128)(2,1)S(1)}, bf16[512,768]{1,0:T(8,128)(2,1)S(1)}, u32[]{:S(2)}, u32[]{:S(2)}) collective-permute-start(bf16[512,768]{1,0:T(8,128)(2,1)S(1)} %get-tuple-element.118), channel_id=1, source_target_pairs={{0,1},{3,2},{4,5},{7,6},{8,9},{11,10},{12,13},{15,14},{16,17},{19,... | collective-permute-start | bytes 2359304 | tf_op jit(solution)/shard_map/ppermute | solution.py:406
  750.1 11.7 %collective-permute-done.25 = bf16[512,768]{1,0:T(8,128)(2,1)S(1)} collective-permute-done((bf16[512,768]{1,0:T(8,128)(2,1)S(1)}, bf16[512,768]{1,0:T(8,128)(2,1)S(1)}, u32[]{:S(2)}, u32[]{:S(2)}) %collective-permute-start.25) | collective-permute-done | bytes 786464 | tf_op jit(solution)/shard_map/ppermute | solution.py:406
  766.2 9.3 %collective-permute-done.36 = bf16[3,2,96,384]{3,2,1,0:T(8,128)(2,1)S(1)} collective-permute-done((bf16[3,2,96,384]{3,2,1,0:T(8,128)(2,1)S(1)}, bf16[3,2,96,384]{3,2,1,0:T(8,128)(2,1)S(1)}, u32[]{:S(2)}, u32[]{:S(2)}) %collective-permute-start.36) | collective-permute-done | bytes 442400 | tf_op jit(solution)/shard_map/ppermute | solution.py:221
  775.5 5.0 collective-permute-start.26
  783.2 13.0 %collective-permute-done.26 = bf16[512,768]{1,0:T(8,128)(2,1)S(1)} collective-permute-done((bf16[512,768]{1,0:T(8,128)(2,1)S(1)}, bf16[512,768]{1,0:T(8,128)(2,1)S(1)}, u32[]{:S(2)}, u32[]{:S(2)}) %collective-permute-start.26) | collective-permute-done | bytes 786464 | tf_op jit(solution)/shard_map/ppermute | solution.py:406
  797.9 7.1 collective-permute-start.27
  812.2 6.7 collective-permute-done.29
  831.6 24.9 %collective-permute-done.31 = f32[20,768]{1,0:T(8,128)S(1)} collective-permute-done((f32[20,768]{1,0:T(8,128)S(1)}, f32[20,768]{1,0:T(8,128)S(1)}, u32[]{:S(2)}, u32[]{:S(2)}) %collective-permute-start.31) | collective-permute-done | bytes 61472 | tf_op jit(solution)/shard_map/ppermute | solution.py:221
  882.7 4.9 collective-permute-done.45
  892.0 19.8 %collective-permute-done.46 = bf16[2,96,192]{1,2,0:T(8,128)(2,1)S(1)} collective-permute-done((bf16[2,96,192]{1,2,0:T(8,128)(2,1)S(1)}, bf16[2,96,192]{1,2,0:T(8,128)(2,1)S(1)}, u32[]{:S(2)}, u32[]{:S(2)}) %collective-permute-start.46) | collective-permute-done | bytes 73760 | tf_op jit(solution)/shard_map/ppermute | solution.py:221
  (393 shorter events, 184.7 us)
Async XLA Ops:
  12.6 51.4 %collective-permute-start.11 = (bf16[512,768]{1,0:T(8,128)(2,1)S(1)}, bf16[512,768]{1,0:T(8,128)(2,1)}, u32[]{:S(2)}, u32[]{:S(2)}) collective-permute-start(bf16[512,768]{1,0:T(8,128)(2,1)S(1)} %add_convert_fusion.8), channel_id=1, source_target_pairs={{0,1},{1,2},{2,3},{4,5},{5,6},{6,7},{8,9},{9,10},{10,11},{12,13},{... | collective-permute-start | bytes 2359304 | tf_op jit(solution)/shard_map/ppermute | solution.py:406
  19.1 28.2 %collective-permute-start.1 = (bf16[384,384]{1,0:T(8,128)(2,1)}, bf16[384,384]{1,0:T(8,128)(2,1)S(1)}, u32[]{:S(2)}, u32[]{:S(2)}) collective-permute-start(bf16[384,384]{1,0:T(8,128)(2,1)} %pad_maximum_fusion.11), channel_id=1, source_target_pairs={{0,2},{1,3},{2,0},{3,1},{4,6},{5,7},{6,4},{7,5},{8,10},{9,11},{10,... | collective-permute-start | bytes 884744 | tf_op jit(solution)/shard_map/ppermute | solution.py:221
  22.1 37.6 %collective-permute-start.20 = (bf16[384,768]{1,0:T(8,128)(2,1)S(1)}, bf16[384,768]{1,0:T(8,128)(2,1)S(1)}, u32[]{:S(2)}, u32[]{:S(2)}) collective-permute-start(bf16[384,768]{1,0:T(8,128)(2,1)S(1)} %pad_maximum_fusion.6), channel_id=1, source_target_pairs={{0,2},{1,3},{2,0},{3,1},{4,6},{5,7},{6,4},{7,5},{8,10},{9,11},{10,... | collective-permute-start | bytes 1769480 | tf_op jit(solution)/shard_map/ppermute | solution.py:221
  51.3 35.2 %collective-permute-start.16 = (bf16[432,768]{1,0:T(8,128)(2,1)S(1)}, bf16[432,768]{1,0:T(8,128)(2,1)S(1)}, u32[]{:S(2)}, u32[]{:S(2)}) collective-permute-start(bf16[432,768]{1,0:T(8,128)(2,1)S(1)} %pad_maximum_fusion.4), channel_id=1, source_target_pairs={{0,8},{4,12},{8,0},{12,4},{16,24},{20,28},{24,16},{28,20},{1,9},{5... | collective-permute-start | bytes 1990664 | tf_op jit(solution)/shard_map/ppermute | solution.py:221
  59.7 26.8 %collective-permute-start.21 = (bf16[432,768]{1,0:T(8,128)(2,1)S(1)}, bf16[432,768]{1,0:T(8,128)(2,1)S(1)}, u32[]{:S(2)}, u32[]{:S(2)}) collective-permute-start(bf16[432,768]{1,0:T(8,128)(2,1)S(1)} %pad_maximum_fusion.5), channel_id=1, source_target_pairs={{0,16},{4,20},{8,24},{12,28},{16,0},{20,4},{24,8},{28,12},{1,17},{... | collective-permute-start | bytes 1990664 | tf_op jit(solution)/shard_map/ppermute | solution.py:221
  61.4 24.6 %collective-permute-start.3 = (bf16[288,768]{1,0:T(8,128)(2,1)S(1)}, bf16[288,768]{1,0:T(8,128)(2,1)S(1)}, u32[]{:S(2)}, u32[]{:S(2)}) collective-permute-start(bf16[288,768]{1,0:T(8,128)(2,1)S(1)} %pad_maximum_fusion.9.refs_0_), channel_id=1, source_target_pairs={{0,16},{4,20},{8,24},{12,28},{16,0},{20,4},{24,8},{28,12},{1,17},{... | collective-permute-start | bytes 1327112 | tf_op jit(solution)/shard_map/ppermute | solution.py:221
  64.1 29.8 %collective-permute-start.10 = (bf16[512,768]{1,0:T(8,128)(2,1)S(1)}, bf16[512,768]{1,0:T(8,128)(2,1)}, u32[]{:S(2)}, u32[]{:S(2)}) collective-permute-start(bf16[512,768]{1,0:T(8,128)(2,1)S(1)} %add_convert_fusion.8), channel_id=1, source_target_pairs={{1,0},{2,1},{3,2},{5,4},{6,5},{7,6},{9,8},{10,9},{11,10},{13,12},{... | collective-permute-start | bytes 2359304 | tf_op jit(solution)/shard_map/ppermute | solution.py:406
  93.9 116.4 %collective-permute-start.12 = (bf16[512,768]{1,0:T(8,128)(2,1)}, bf16[512,768]{1,0:T(8,128)(2,1)S(1)}, u32[]{:S(2)}, u32[]{:S(2)}) collective-permute-start(bf16[512,768]{1,0:T(8,128)(2,1)} %collective-permute-done.11), channel_id=1, source_target_pairs={{1,2},{2,3},{5,6},{6,7},{9,10},{10,11},{13,14},{14,15},{17,18},{18... | collective-permute-start | bytes 2359304 | tf_op jit(solution)/shard_map/ppermute | solution.py:406
  94.6 116.3 %collective-permute-start.13 = (bf16[512,768]{1,0:T(8,128)(2,1)}, bf16[512,768]{1,0:T(8,128)(2,1)S(1)}, u32[]{:S(2)}, u32[]{:S(2)}) collective-permute-start(bf16[512,768]{1,0:T(8,128)(2,1)} %collective-permute-done.10), channel_id=1, source_target_pairs={{1,0},{2,1},{5,4},{6,5},{9,8},{10,9},{13,12},{14,13},{17,16},{18,1... | collective-permute-start | bytes 2359304 | tf_op jit(solution)/shard_map/ppermute | solution.py:406
  95.9 217.5 %collective-permute-start.18 = (bf16[864,768]{1,0:T(8,128)(2,1)}, bf16[864,768]{1,0:T(8,128)(2,1)}, u32[]{:S(2)}, u32[]{:S(2)}) collective-permute-start(bf16[864,768]{1,0:T(8,128)(2,1)} %constant_dynamic-update-slice_fusion.refs_0_), channel_id=1, source_target_pairs={{0,4},{4,0},{8,12},{12,8},{16,20},{20,16},{24,28},{28,24},{1,5},{5... | collective-permute-start | bytes 3981320 | tf_op jit(solution)/shard_map/ppermute | solution.py:221
  96.0 148.9 %collective-permute-start.17 = (bf16[864,768]{1,0:T(8,128)(2,1)}, bf16[864,768]{1,0:T(8,128)(2,1)}, u32[]{:S(2)}, u32[]{:S(2)}) collective-permute-start(bf16[864,768]{1,0:T(8,128)(2,1)} %constant_dynamic-update-slice_fusion.refs_0_), channel_id=1, source_target_pairs={{0,16},{4,20},{8,24},{12,28},{16,0},{20,4},{24,8},{28,12},{1,17},{... | collective-permute-start | bytes 3981320 | tf_op jit(solution)/shard_map/ppermute | solution.py:221
  97.6 215.9 %collective-permute-start.23 = (bf16[864,768]{1,0:T(8,128)(2,1)}, bf16[864,768]{1,0:T(8,128)(2,1)}, u32[]{:S(2)}, u32[]{:S(2)}) collective-permute-start(bf16[864,768]{1,0:T(8,128)(2,1)} %pad_maximum_fusion.3.refs_4_), channel_id=1, source_target_pairs={{0,4},{4,0},{8,12},{12,8},{16,20},{20,16},{24,28},{28,24},{1,5},{5... | collective-permute-start | bytes 3981320 | tf_op jit(solution)/shard_map/ppermute | solution.py:221
  210.3 34.7 %collective-permute-start.22 = (bf16[864,768]{1,0:T(8,128)(2,1)}, bf16[864,768]{1,0:T(8,128)(2,1)}, u32[]{:S(2)}, u32[]{:S(2)}) collective-permute-start(bf16[864,768]{1,0:T(8,128)(2,1)} %pad_maximum_fusion.3.refs_4_), channel_id=1, source_target_pairs={{0,8},{4,12},{8,0},{12,4},{16,24},{20,28},{24,16},{28,20},{1,9},{5... | collective-permute-start | bytes 3981320 | tf_op jit(solution)/shard_map/ppermute | solution.py:221
  211.0 30.9 %collective-permute-start.14 = (bf16[512,768]{1,0:T(8,128)(2,1)S(1)}, bf16[512,768]{1,0:T(8,128)(2,1)S(1)}, u32[]{:S(2)}, u32[]{:S(2)}) collective-permute-start(bf16[512,768]{1,0:T(8,128)(2,1)S(1)} %broadcast_select_fusion.1), channel_id=1, source_target_pairs={{1,0},{2,3},{5,4},{6,7},{9,8},{10,11},{13,12},{14,15},{17,16},{18,... | collective-permute-start | bytes 2359304 | tf_op jit(solution)/shard_map/ppermute | solution.py:406
  244.9 68.6 %collective-permute-start.19 = (bf16[864,768]{1,0:T(8,128)(2,1)}, bf16[864,768]{1,0:T(8,128)(2,1)}, u32[]{:S(2)}, u32[]{:S(2)}) collective-permute-start(bf16[864,768]{1,0:T(8,128)(2,1)} %collective-permute-done.17.refs_1_), channel_id=1, source_target_pairs={{0,4},{4,0},{8,12},{12,8},{16,20},{20,16},{24,28},{28,24},{1,5},{5... | collective-permute-start | bytes 3981320 | tf_op jit(solution)/shard_map/ppermute | solution.py:221
  245.0 68.5 %collective-permute-start.24 = (bf16[864,768]{1,0:T(8,128)(2,1)}, bf16[864,768]{1,0:T(8,128)(2,1)}, u32[]{:S(2)}, u32[]{:S(2)}) collective-permute-start(bf16[864,768]{1,0:T(8,128)(2,1)} %collective-permute-done.22.refs_5_), channel_id=1, source_target_pairs={{0,4},{4,0},{8,12},{12,8},{16,20},{20,16},{24,28},{28,24},{1,5},{5... | collective-permute-start | bytes 3981320 | tf_op jit(solution)/shard_map/ppermute | solution.py:221
  734.8 27.0 %collective-permute-start.25 = (bf16[512,768]{1,0:T(8,128)(2,1)S(1)}, bf16[512,768]{1,0:T(8,128)(2,1)S(1)}, u32[]{:S(2)}, u32[]{:S(2)}) collective-permute-start(bf16[512,768]{1,0:T(8,128)(2,1)S(1)} %get-tuple-element.118), channel_id=1, source_target_pairs={{0,1},{3,2},{4,5},{7,6},{8,9},{11,10},{12,13},{15,14},{16,17},{19,... | collective-permute-start | bytes 2359304 | tf_op jit(solution)/shard_map/ppermute | solution.py:406
  745.6 64.2 %collective-permute-start.48 = (bf16[4,2,2,96,768]{4,3,0,2,1:T(8,128)(2,1)S(1)}, bf16[4,2,2,96,768]{4,3,0,2,1:T(8,128)(2,1)S(1)}, u32[]{:S(2)}, u32[]{:S(2)}) collective-permute-start(bf16[4,2,2,96,768]{4,3,0,2,1:T(8,128)(2,1)S(1)} %bitcast.224), channel_id=1, source_target_pairs={{0,4},{4,0},{8,12},{12,8},{16,20},{20,16},{24,28},{28,24},{1,5},{5... | collective-permute-start | bytes 7077896 | tf_op jit(solution)/shard_map/ppermute | solution.py:221
  747.0 76.8 %collective-permute-start.43 = (bf16[5,2,2,96,768]{4,3,2,1,0:T(8,128)(2,1)S(1)}, bf16[5,2,2,96,768]{4,3,2,1,0:T(8,128)(2,1)S(1)}, u32[]{:S(2)}, u32[]{:S(2)}) collective-permute-start(bf16[5,2,2,96,768]{4,3,2,1,0:T(8,128)(2,1)S(1)} %fusion.29), channel_id=1, source_target_pairs={{0,4},{4,0},{8,12},{12,8},{16,20},{20,16},{24,28},{28,24},{1,5},{5... | collective-permute-start | bytes 8847368 | tf_op jit(solution)/shard_map/ppermute | solution.py:221
  797.9 24.3 %collective-permute-start.27 = (bf16[512,768]{1,0:T(8,128)(2,1)S(1)}, bf16[512,768]{1,0:T(8,128)(2,1)S(1)}, u32[]{:S(2)}, u32[]{:S(2)}) collective-permute-start(bf16[512,768]{1,0:T(8,128)(2,1)S(1)} %select_convert_fusion), channel_id=1, source_target_pairs={{0,1},{1,2},{2,3},{4,5},{5,6},{6,7},{8,9},{9,10},{10,11},{12,13},{... | collective-permute-start | bytes 2359304 | tf_op jit(solution)/shard_map/ppermute | solution.py:406
  805.8 51.3 %collective-permute-start.41 = (bf16[3,96,384]{2,1,0:T(8,128)(2,1)}, bf16[3,96,384]{2,1,0:T(8,128)(2,1)}, u32[]{:S(2)}, u32[]{:S(2)}) collective-permute-start(bf16[3,96,384]{2,1,0:T(8,128)(2,1)} %select_convert_fusion.1), channel_id=1, source_target_pairs={{0,2},{1,3},{2,0},{3,1},{4,6},{5,7},{6,4},{7,5},{8,10},{9,11},{10,... | collective-permute-start | bytes 663560 | tf_op jit(solution)/shard_map/ppermute | solution.py:221
  811.7 59.3 %collective-permute-start.49 = (bf16[4,2,96,768]{3,2,0,1:T(8,128)(2,1)}, bf16[4,2,96,768]{3,2,0,1:T(8,128)(2,1)}, u32[]{:S(2)}, u32[]{:S(2)}) collective-permute-start(bf16[4,2,96,768]{3,2,0,1:T(8,128)(2,1)} %dynamic-slice_bitcast_fusion.1), channel_id=1, source_target_pairs={{0,16},{4,20},{8,24},{12,28},{16,0},{20,4},{24,8},{28,12},{1,17},{... | collective-permute-start | bytes 3538952 | tf_op jit(solution)/shard_map/ppermute | solution.py:221
  826.0 48.3 %collective-permute-start.44 = (bf16[5,2,96,768]{3,2,1,0:T(8,128)(2,1)}, bf16[5,2,96,768]{3,2,1,0:T(8,128)(2,1)}, u32[]{:S(2)}, u32[]{:S(2)}) collective-permute-start(bf16[5,2,96,768]{3,2,1,0:T(8,128)(2,1)} %dynamic-slice_bitcast_fusion), channel_id=1, source_target_pairs={{0,8},{4,12},{8,0},{12,4},{16,24},{20,28},{24,16},{28,20},{1,9},{5... | collective-permute-start | bytes 4423688 | tf_op jit(solution)/shard_map/ppermute | solution.py:221
  830.9 25.7 %collective-permute-start.31 = (f32[20,768]{1,0:T(8,128)S(1)}, f32[20,768]{1,0:T(8,128)S(1)}, u32[]{:S(2)}, u32[]{:S(2)}) collective-permute-start(f32[20,768]{1,0:T(8,128)S(1)} %add.462), channel_id=1, source_target_pairs={{0,8},{4,12},{8,0},{12,4},{16,24},{20,28},{24,16},{28,20},{1,9},{5... | collective-permute-start | bytes 184328 | tf_op jit(solution)/shard_map/ppermute | solution.py:221
  (101 other events, 2028.3 us)

commit v3 on v2

v3 whole, which is shorter than its diff:
```python
import functools

import jax
import jax.numpy as jnp
from jax import lax
from jax.experimental import pallas as pl
from jax.experimental.pallas import tpu as pltpu
from jax.sharding import PartitionSpec as P

D = 768
HEADS = 12
HEAD_DIM = 64
FF = 3072
MAXLEN = 2048
PAIR = 2 * HEAD_DIM
PAIRS = HEADS // 2
VMEM_LIMIT = 58 << 20

far_below = -1e30
epsilon = 1e-05
score_scale = HEAD_DIM ** (-0.5)
low = jnp.bfloat16
full = jnp.float32
both = ("dp", "mp")


def norm_stats(values):
    center = values - jnp.mean(values, axis=-1, keepdims=True)
    spread = jnp.mean(center * center, axis=-1, keepdims=True)
    inverse = lax.rsqrt(spread + epsilon)
    return center * inverse, inverse


def norm_back(unit, inverse, gain_row, grad):
    scaled = grad * gain_row
    mean_scaled = jnp.mean(scaled, axis=-1, keepdims=True)
    mean_unit = jnp.mean(scaled * unit, axis=-1, keepdims=True)
    return (
        inverse * (scaled - mean_scaled - unit * mean_unit),
        jnp.sum(grad * unit, axis=0),
        jnp.sum(grad, axis=0),
    )


def dot_of(left_side, right_side, left_dim, right_dim):
    return lax.dot_general(
        left_side,
        right_side,
        (((left_dim,), (right_dim,)), ((), ())),
        preferred_element_type=full,
    )


def first_half(shape):
    return lax.broadcasted_iota(jnp.int32, shape, len(shape) - 1) < HEAD_DIM


def forward_kernel(first, scalars, q_ref, *refs):
    count = 2
    key_refs, value_refs = refs[:count], refs[count : 2 * count]
    refs = refs[2 * count :]
    if not first:
        top_in, sum_in, acc_in = refs[:3]
        refs = refs[3:]
    rows = q_ref.shape[0]
    keys = key_refs[0].shape[0]
    place = lax.broadcasted_iota(jnp.int32, (1, keys), 1)
    q_pair = q_ref[...]
    lower = first_half((rows, PAIR))
    parts = []
    for half in range(2):
        kept = lower if half == 0 else jnp.logical_not(lower)
        q_half = jnp.where(kept, q_pair, jnp.zeros_like(q_pair))
        scores = []
        for n in range(count):
            bias = jnp.where(place + scalars[n] * keys < scalars[count], 0.0, far_below)
            scores.append(dot_of(q_half, key_refs[n][...], 1, 1) + bias)
        highest = functools.reduce(
            jnp.maximum, [jnp.max(score, axis=-1, keepdims=True) for score in scores]
        )
        totals = jnp.zeros_like(highest)
        mixed = jnp.zeros((rows, PAIR), full)
        for n in range(count):
            exp_scores = jnp.exp(scores[n] - highest)
            totals = totals + jnp.sum(exp_scores, axis=-1, keepdims=True)
            mixed = mixed + dot_of(exp_scores.astype(low), value_refs[n][...], 1, 0)
        parts.append((highest, totals, mixed))
    top = jnp.where(lower, parts[0][0], parts[1][0])
    total = jnp.where(lower, parts[0][1], parts[1][1])
    mixed = jnp.where(lower, parts[0][2], parts[1][2])
    if first:
        top_ref, sum_ref, acc_ref = refs
        top_ref[...] = top
        sum_ref[...] = total
        acc_ref[...] = mixed
    else:
        out_ref, log_ref = refs
        highest = jnp.maximum(top, top_in[...])
        here = jnp.exp(top - highest)
        before = jnp.exp(top_in[...] - highest)
        total = total * here + sum_in[...] * before
        out_ref[...] = (mixed * here + acc_in[...] * before) / total
        log_ref[...] = highest + jnp.log(total)


def attend_forward(queries, keys, values, scalars, state):
    rows, total = queries.shape[0], keys[0].shape[0]
    first = state is None
    pair_rows = lambda count: pl.BlockSpec((count, PAIR), lambda i, n: (0, i))
    wide = jax.ShapeDtypeStruct((rows, D), full)
    carried = () if first else state
    return pl.pallas_call(
        functools.partial(forward_kernel, first),
        out_shape=(wide,) * (3 if first else 2),
        grid_spec=pltpu.PrefetchScalarGridSpec(
            num_scalar_prefetch=1,
            grid=(PAIRS,),
            in_specs=[pair_rows(rows)]
            + [pair_rows(total)] * (len(keys) + len(values))
            + [pair_rows(rows)] * len(carried),
            out_specs=[pair_rows(rows)] * (3 if first else 2),
        ),
        compiler_params=pltpu.CompilerParams(vmem_limit_bytes=VMEM_LIMIT),
        cost_estimate=pl.CostEstimate(
            flops=8 * rows * total * D * 4,
            bytes_accessed=24 * total * D,
            transcendentals=2 * rows * total * HEADS,
        ),
        name="attend_forward",
    )(scalars, queries, *keys, *values, *carried)


def backward_kernel(
    first,
    last,
    scalars,
    q_ref,
    k_ref,
    v_ref,
    g_ref,
    log_ref,
    delta_ref,
    wk_ref,
    wv_ref,
    *refs
):
    if last:
        wq_ref = refs[0]
        refs = refs[1:]
    if not first:
        dq_in = refs[0]
        refs = refs[1:]
    dq_ref, dk_ref, dv_ref, back_ref, accum = refs
    step = pl.program_id(0)
    rows = q_ref.shape[0]
    keys = k_ref.shape[0]
    limit = scalars[1] - scalars[0] * keys
    q_pair = q_ref[...]
    g_pair = g_ref[...]
    k_pair = k_ref[...]
    v_pair = v_ref[...]
    lower = first_half((rows, PAIR))
    lower_keys = first_half((keys, PAIR))
    place = lax.broadcasted_iota(jnp.int32, (keys, 1), 0)
    bias = jnp.where(place < limit, 0.0, far_below)
    dq = []
    dk = []
    dv = []
    for half in range(2):
        kept = lower if half == 0 else jnp.logical_not(lower)
        q_half = jnp.where(kept, q_pair, jnp.zeros_like(q_pair))
        g_half = jnp.where(kept, g_pair, jnp.zeros_like(g_pair))
        log_row = log_ref[0, half : half + 1, :]
        delta_row = delta_ref[0, half : half + 1, :]
        scores = dot_of(k_pair, q_half, 1, 1) + bias
        probs = jnp.exp(scores - log_row)
        dv.append(dot_of(probs.astype(low), g_pair, 1, 0))
        prob_grad = dot_of(v_pair, g_half, 1, 1)
        score_grad = (probs * (prob_grad - delta_row)).astype(low)
        dk.append(dot_of(score_grad, q_pair, 1, 0))
        dq.append(dot_of(score_grad, k_pair, 0, 0))
    dk_low = jnp.where(lower_keys, dk[0], dk[1]).astype(low)
    dv_low = jnp.where(lower_keys, dv[0], dv[1]).astype(low)
    dk_ref[...] = dk_low
    dv_ref[...] = dv_low
    grads = [dk_low, dv_low]
    weights = [wk_ref[0], wv_ref[0]]
    dq_all = jnp.where(lower, dq[0], dq[1])
    if not first:
        dq_all = dq_all + dq_in[...]
    back = dot_of(jnp.concatenate(grads, axis=1), jnp.concatenate(weights, axis=1), 1, 1)
    if last:
        dq_low = (dq_all * score_scale).astype(low)
        dq_ref[...] = dq_low
        back = back + dot_of(dq_low, wq_ref[0], 1, 1)
    else:
        dq_ref[...] = dq_all

    @pl.when(step == 0)
    def _():
        accum[...] = back

    @pl.when(step > 0)
    def _():
        accum[...] += back

    @pl.when(step == PAIRS - 1)
    def _():
        back_ref[...] = accum[...].astype(back_ref.dtype)


def attend_backward(
    queries, keys, values, grads, logs, deltas, weights, scalars, carried, last
):
    rows, total = queries.shape[0], keys.shape[0]
    first = carried is None
    pair_rows = lambda count: pl.BlockSpec((count, PAIR), lambda i, n: (0, i))
    stats = pl.BlockSpec((1, 2, rows), lambda i, n: (i, 0, 0))
    weight = lambda c: pl.BlockSpec((1, D, PAIR), lambda i, n: (c, 0, i))
    extra = (weights,) * last + (() if first else (carried,))
    extra_specs = [weight(0)] * last + ([] if first else [pair_rows(rows)])
    return pl.pallas_call(
        functools.partial(backward_kernel, first, last),
        out_shape=(
            jax.ShapeDtypeStruct((rows, D), low if last else full),
            jax.ShapeDtypeStruct((total, D), low),
            jax.ShapeDtypeStruct((total, D), low),
            jax.ShapeDtypeStruct((total, D), low if first else full),
        ),
        grid_spec=pltpu.PrefetchScalarGridSpec(
            num_scalar_prefetch=1,
            grid=(PAIRS,),
            in_specs=[
                pair_rows(rows),
                pair_rows(total),
                pair_rows(total),
                pair_rows(rows),
                stats,
                stats,
                weight(1),
                weight(2),
            ]
            + extra_specs,
            out_specs=[
                pair_rows(rows),
                pair_rows(total),
                pair_rows(total),
                pl.BlockSpec((total, D), lambda i, n: (0, 0)),
            ],
            scratch_shapes=[pltpu.VMEM((total, D), full)],
        ),
        compiler_params=pltpu.CompilerParams(vmem_limit_bytes=VMEM_LIMIT),
        cost_estimate=pl.CostEstimate(
            flops=10 * rows * total * D * 4,
            bytes_accessed=16 * total * D,
            transcendentals=rows * total * HEADS,
        ),
        name="attend_backward",
    )(scalars, queries, keys, values, grads, logs, deltas, weights, weights, *extra)


def swap(value, axis, bit):
    count = lax.axis_size(axis)
    return lax.ppermute(value, axis, [(i, i ^ bit) for i in range(count)])


def after(value, *waits):
    return lax.optimization_barrier((value,) + waits)[0]


def outer_bits():
    bits = []
    bit = 2
    while bit < lax.axis_size("dp"):
        bits.append(bit)
        bit *= 2
    return bits


def gather_dp(parts, waits=()):
    bits = outer_bits()
    half = len(bits) // 2
    orders = [bits[half * (n % 2) :] + bits[: half * (n % 2)] for n in range(len(parts))]
    held = [[([0], part)] for part in parts]
    for step in range(len(bits)):
        arrived = []
        for n in range(len(parts)):
            bit = orders[n][step]
            masks = [m for mask, _ in held[n] for m in mask]
            arrays = [array for _, array in held[n]]
            block = jnp.concatenate(arrays) if step else after(arrays[0], *waits)
            arrived.append([(masks, block), ([m ^ bit for m in masks], swap(block, "dp", bit))])
        held = arrived
    return [
        pieces + [([m ^ 1 for m in masks], swap(block, "dp", 1)) for masks, block in pieces]
        for pieces in held
    ]


def canonical_row(me, rank, block, mask, rank_mask, stride, offset):
    if mask is None:
        return offset
    row = (me ^ mask) * block + offset
    if stride:
        row = row + (rank ^ rank_mask) * stride
    return pl.multiple_of(row, 16)


def place_kernel(plan, block, *refs):
    count = len(plan)
    ins = refs[:count]
    outs = refs[count:-1]
    sems = refs[-1]
    me = lax.axis_index("dp")
    rank = lax.axis_index("mp")
    copies = []
    for ref, moves in zip(ins, plan):
        for start, size, which, mask, rank_mask, stride, offset in moves:
            row = canonical_row(me, rank, block, mask, rank_mask, stride, offset)
            copy = pltpu.make_async_copy(
                ref.at[pl.ds(start, size), :],
                outs[which].at[pl.ds(row, size), :],
                sems.at[len(copies)],
            )
            copy.start()
            copies.append(copy)
    for copy in copies:
        copy.wait()


def plan_of(gathered, layouts):
    arrays = []
    plan = []
    for pieces, layout in zip(gathered, layouts):
        rows = sum(size for _, size, *_ in layout)
        for masks, array in pieces:
            moves = []
            for j, mask in enumerate(masks):
                for start, size, which, rank_mask, stride, offset in layout:
                    moves.append((j * rows + start, size, which, mask, rank_mask, stride, offset))
            arrays.append(array)
            plan.append(moves)
    return arrays, plan


def place(arrays, plan, block, shapes):
    moved = sum(array.size for array in arrays) * 4
    return pl.pallas_call(
        functools.partial(place_kernel, plan, block),
        out_shape=[jax.ShapeDtypeStruct(shape, low) for shape in shapes],
        in_specs=[pl.BlockSpec(memory_space=pl.ANY)] * len(arrays),
        out_specs=[pl.BlockSpec(memory_space=pltpu.VMEM)] * len(shapes),
        scratch_shapes=[pltpu.SemaphoreType.DMA((sum(len(moves) for moves in plan),))],
        compiler_params=pltpu.CompilerParams(vmem_limit_bytes=VMEM_LIMIT),
        cost_estimate=pl.CostEstimate(flops=0, bytes_accessed=moved, transcendentals=0),
        name="place",
    )(*arrays)


def middle_kernel(plan, block, total, *refs):
    limit_ref, vector_ref = refs[:2]
    token_hbm, mixed_hbm, log_hbm, cot_hbm, teach_hbm = refs[2:7]
    pieces = refs[7 : 7 + total]
    (
        out_hbm,
        final_hbm,
        act_hbm,
        pre_hbm,
        second_hbm,
        middle_low_hbm,
        attended_hbm,
        middle_hbm,
        grad_hbm,
        delta_ref,
        log_ref,
        sum_ref,
    ) = refs[7 + total : 19 + total]
    (
        token,
        mixed,
        logs,
        cot,
        teach,
        up,
        down,
        proj,
        act,
        pre,
        slope,
        second,
        attended,
        middle,
        final,
        out,
        final_low,
        middle_low,
        grad,
        accum,
        in_sems,
        weight_sems,
        out_sems,
    ) = refs[19 + total :]
    targets = (up, down, proj)
    rows = token.shape[0]
    me = lax.axis_index("dp")
    rank = lax.axis_index("mp")

    def fetch(ref, scratch, n):
        copy = pltpu.make_async_copy(ref, scratch, in_sems.at[n])
        copy.start()
        return copy

    def send(scratch, ref, n):
        copy = pltpu.make_async_copy(scratch, ref, out_sems.at[n])
        copy.start()
        return copy

    gets = [
        fetch(token_hbm, token, 0),
        fetch(mixed_hbm, mixed, 1),
        fetch(log_hbm, logs, 2),
        fetch(cot_hbm, cot, 3),
        fetch(teach_hbm, teach, 4),
    ]
    loads = {0: [], 1: [], 2: []}
    number = 0
    for want in (2, 0, 1):
        for ref, moves in zip(pieces, plan):
            for start, size, which, mask, rank_mask, stride, offset in moves:
                if which != want:
                    continue
                row = canonical_row(me, rank, block, mask, rank_mask, stride, offset)
                copy = pltpu.make_async_copy(
                    ref.at[pl.ds(start, size), :],
                    targets[which].at[pl.ds(row, size), :],
                    weight_sems.at[number],
                )
                copy.start()
                loads[which].append(copy)
                number += 1

    table_row = vector_ref[0:1, :]
    out_bias = vector_ref[1:2, :]
    gain = vector_ref[2:3, :]
    shift = vector_ref[3:4, :]
    down_bias = vector_ref[4:5, :]
    weight = vector_ref[5:6, :]
    gets[0].wait()
    gets[1].wait()
    attended[...] = mixed[...].astype(low)
    puts = [send(attended, attended_hbm, 0)]
    for copy in loads[2]:
        copy.wait()
    state = token[...].astype(full) + table_row + out_bias
    state = state + dot_of(attended[...], proj[...], 1, 1)
    middle[...] = state
    unit, _ = norm_stats(state)
    second[...] = (unit * gain + shift).astype(low)
    puts.append(send(second, second_hbm, 1))
    accum[...] = jnp.zeros((rows, D), full)
    for copy in loads[0]:
        copy.wait()
    for copy in loads[1]:
        copy.wait()

    def forward(m, _):
        place = pl.ds(pl.multiple_of(m * D, D), D)
        value = dot_of(second[...], up[place, :], 1, 0) + vector_ref[pl.ds(8 + m, 1), :]
        cumulative = 0.5 + 0.5 * lax.erf(value * (0.5**0.5))
        act[m] = (value * cumulative).astype(low)
        slope[m] = cumulative + value * jnp.exp(-0.5 * value * value) * 0.3989422804014327
        accum[...] += dot_of(act[m], down[place, :], 1, 1)
        return 0

    lax.fori_loop(0, FF // D, forward, 0)
    puts.append(send(act, act_hbm, 2))
    final_state = middle[...] + accum[...] + down_bias
    out[...] = final_state.astype(low)
    puts.append(send(out, out_hbm, 3))
    gets[3].wait()
    gets[4].wait()
    place = lax.broadcasted_iota(jnp.int32, (rows, 1), 0)
    grads = cot[...].astype(full) + weight * (final_state - teach[...].astype(full))
    grads = jnp.where(place < limit_ref[0], grads, 0.0)
    final[...] = grads
    final_low[...] = grads.astype(low)
    puts.append(send(final_low, final_hbm, 4))
    sum_ref[3:4, :] = jnp.sum(grads, axis=0, keepdims=True)
    accum[...] = jnp.zeros((rows, D), full)

    def backward(m, _):
        place = pl.ds(pl.multiple_of(m * D, D), D)
        value = slope[m] * dot_of(final_low[...], down[place, :], 1, 0)
        value = value.astype(low)
        pre[m] = value
        sum_ref[pl.ds(8 + m, 1), :] = jnp.sum(value.astype(full), axis=0, keepdims=True)
        accum[...] += dot_of(value, up[place, :], 1, 1)
        return 0

    lax.fori_loop(0, FF // D, backward, 0)
    puts.append(send(pre, pre_hbm, 5))
    unit, inverse = norm_stats(middle[...])
    second_grad = accum[...]
    sum_ref[0:1, :] = jnp.sum(second_grad * unit, axis=0, keepdims=True)
    sum_ref[1:2, :] = jnp.sum(second_grad, axis=0, keepdims=True)
    scaled = second_grad * gain
    mean_scaled = jnp.mean(scaled, axis=-1, keepdims=True)
    mean_unit = jnp.mean(scaled * unit, axis=-1, keepdims=True)
    total_grad = final[...] + inverse * (scaled - mean_scaled - unit * mean_unit)
    middle[...] = total_grad
    puts.append(send(middle, middle_hbm, 6))
    middle_low[...] = total_grad.astype(low)
    puts.append(send(middle_low, middle_low_hbm, 7))
    sum_ref[2:3, :] = jnp.sum(total_grad, axis=0, keepdims=True)
    attended_grad = dot_of(middle_low[...], proj[...], 1, 0).astype(low)
    grad[...] = attended_grad
    puts.append(send(grad, grad_hbm, 8))
    gets[2].wait()
    head = lax.broadcasted_iota(jnp.int32, (16, D), 0)
    lane = lax.broadcasted_iota(jnp.int32, (16, D), 1)
    member = jnp.where(lane // HEAD_DIM == head, 1.0, 0.0)
    leader = jnp.where(lane == head * HEAD_DIM, 1.0, 0.0)
    exact = functools.partial(
        lax.dot_general,
        dimension_numbers=(((1,), (1,)), ((), ())),
        precision=lax.Precision.HIGHEST,
        preferred_element_type=full,
    )
    deltas = exact(member, attended_grad.astype(full) * mixed[...])
    tops = exact(leader, logs[...])
    for pair in range(PAIRS):
        delta_ref[pair] = deltas[2 * pair : 2 * pair + 2]
        log_ref[pair] = tops[2 * pair : 2 * pair + 2]
    for copy in puts:
        copy.wait()


def middle_call(limit, vectors, tokens, mixed, logs, cot, teach, arrays, plan, block):
    rows = tokens.shape[0]
    hidden = FF // D
    narrow = jax.ShapeDtypeStruct((rows, D), low)
    wide = jax.ShapeDtypeStruct((rows, D), full)
    many = jax.ShapeDtypeStruct((hidden, rows, D), low)
    stats = jax.ShapeDtypeStruct((PAIRS, 2, rows), full)
    anywhere = pl.BlockSpec(memory_space=pl.ANY)
    inside = pl.BlockSpec(memory_space=pltpu.VMEM)
    moves = sum(len(part) for part in plan)
    return pl.pallas_call(
        functools.partial(middle_kernel, plan, block, len(arrays)),
        out_shape=(
            narrow,
            narrow,
            many,
            many,
            narrow,
            narrow,
            narrow,
            wide,
            narrow,
            stats,
            stats,
            jax.ShapeDtypeStruct((8 + 8, D), full),
        ),
        in_specs=[pl.BlockSpec(memory_space=pltpu.SMEM), inside]
        + [anywhere] * (5 + len(arrays)),
        out_specs=[anywhere] * 9 + [inside] * 3,
        scratch_shapes=[
            pltpu.VMEM((rows, D), low),
            pltpu.VMEM((rows, D), full),
            pltpu.VMEM((rows, D), full),
            pltpu.VMEM((rows, D), low),
            pltpu.VMEM((rows, D), low),
            pltpu.VMEM((FF, D), low),
            pltpu.VMEM((FF, D), low),
            pltpu.VMEM((D, D), low),
            pltpu.VMEM((hidden, rows, D), low),
            pltpu.VMEM((hidden, rows, D), low),
            pltpu.VMEM((hidden, rows, D), full),
            pltpu.VMEM((rows, D), low),
            pltpu.VMEM((rows, D), low),
            pltpu.VMEM((rows, D), full),
            pltpu.VMEM((rows, D), full),
            pltpu.VMEM((rows, D), low),
            pltpu.VMEM((rows, D), low),
            pltpu.VMEM((rows, D), low),
            pltpu.VMEM((rows, D), low),
            pltpu.VMEM((rows, D), full),
            pltpu.SemaphoreType.DMA((5,)),
            pltpu.SemaphoreType.DMA((moves,)),
            pltpu.SemaphoreType.DMA((9,)),
        ],
        compiler_params=pltpu.CompilerParams(vmem_limit_bytes=VMEM_LIMIT),
        cost_estimate=pl.CostEstimate(
            flops=20 * rows * D * FF, bytes_accessed=30 << 20, transcendentals=2 * rows * FF
        ),
        name="middle",
    )(limit, vectors, tokens, mixed, logs, cot, teach, *arrays)


def feed_grad_kernel(
    final_ref, act_ref, second_ref, pre_ref, middle_ref, attended_ref, *refs
):
    down_keep, down_send, up_keep, up_send, left, right = refs
    block = down_keep.shape[2]
    m = pl.program_id(0)
    even = lax.axis_index("dp") % 2 == 0

    @pl.when(m == 0)
    def _():
        left[...] = final_ref[...].T
        right[...] = second_ref[...].T

    def store(value, keep, send, index):
        for outer in range(down_keep.shape[1]):
            first = value[2 * outer * block : (2 * outer + 1) * block]
            other = value[(2 * outer + 1) * block : (2 * outer + 2) * block]
            keep[index, outer] = jnp.where(even, first, other).astype(low)
            send[index, outer] = jnp.where(even, other, first).astype(low)

    @pl.when(m < FF // D)
    def _():
        store(dot_of(left[...], act_ref[0], 1, 0), down_keep, down_send, 0)
        store(dot_of(right[...], pre_ref[0], 1, 0), up_keep, up_send, 0)

    @pl.when(m == FF // D)
    def _():
        store(dot_of(middle_ref[...].T, attended_ref[...], 1, 0), up_keep, up_send, 0)


def feed_grads(final_low, act, second, pre, middle_low, attended, dp):
    rows = final_low.shape[0]
    hidden = FF // D
    whole = pl.BlockSpec((rows, D), lambda m: (0, 0))
    last = hidden - 1
    slice_of = pl.BlockSpec((1, rows, D), lambda m: (jnp.minimum(m, last), 0, 0))
    shape = (hidden, dp // 2, D // dp, D)
    longer = (hidden + 1,) + shape[1:]
    down_spec = pl.BlockSpec((1,) + shape[1:], lambda m: (jnp.minimum(m, last), 0, 0, 0))
    up_spec = pl.BlockSpec((1,) + shape[1:], lambda m: (m, 0, 0, 0))
    return pl.pallas_call(
        feed_grad_kernel,
        out_shape=[jax.ShapeDtypeStruct(shape, low)] * 2
        + [jax.ShapeDtypeStruct(longer, low)] * 2,
        grid=(hidden + 1,),
        in_specs=[whole, slice_of, whole, slice_of, whole, whole],
        out_specs=[down_spec, down_spec, up_spec, up_spec],
        scratch_shapes=[pltpu.VMEM((D, rows), low)] * 2,
        compiler_params=pltpu.CompilerParams(vmem_limit_bytes=VMEM_LIMIT),
        cost_estimate=pl.CostEstimate(
            flops=10 * rows * D * FF, bytes_accessed=20 << 20, transcendentals=0
        ),
        name="feed_grads",
    )(final_low, act, second, pre, middle_low, attended)


def qkv_grad_kernel(count, *refs):
    chunk_refs = refs[:count]
    query_ref = refs[count]
    key_refs = refs[count + 1 : 2 * count + 1]
    value_refs = refs[2 * count + 1 : 3 * count + 1]
    keep_ref, send_ref, sum_ref, turned = refs[3 * count + 1 :]
    block = keep_ref.shape[2]
    rows = query_ref.shape[0]
    c = pl.program_id(0)
    even = lax.axis_index("dp") % 2 == 0
    ones = jnp.ones((16, rows), low)

    def store(value):
        for outer in range(keep_ref.shape[1]):
            first = value[2 * outer * block : (2 * outer + 1) * block]
            other = value[(2 * outer + 1) * block : (2 * outer + 2) * block]
            keep_ref[0, outer] = jnp.where(even, first, other).astype(low)
            send_ref[0, outer] = jnp.where(even, other, first).astype(low)

    @pl.when(c == 0)
    def _():
        for n in range(count):
            turned[n] = chunk_refs[n][...].T
        store(dot_of(turned[0], query_ref[...], 1, 0))
        sum_ref[0:8, :] = dot_of(ones, query_ref[...], 1, 0)[0:8]

    def many(sources):
        value = dot_of(turned[0], sources[0][...], 1, 0)
        for n in range(1, count):
            value = value + dot_of(turned[n], sources[n][...], 1, 0)
        store(value)

    @pl.when(c == 1)
    def _():
        many(key_refs)

    @pl.when(c == 2)
    def _():
        many(value_refs)
        value = dot_of(ones, value_refs[0][...], 1, 0)
        for n in range(1, count):
            value = value + dot_of(ones, value_refs[n][...], 1, 0)
        sum_ref[8:16, :] = value[0:8]


def qkv_grads(chunks, query_grad, key_grads, value_grads, dp):
    rows = query_grad.shape[0]
    count = len(chunks)
    whole = pl.BlockSpec((rows, D), lambda c: (0, 0))
    shape = (3, dp // 2, D // dp, D)
    part = pl.BlockSpec((1,) + shape[1:], lambda c: (c, 0, 0, 0))
    return pl.pallas_call(
        functools.partial(qkv_grad_kernel, count),
        out_shape=[jax.ShapeDtypeStruct(shape, low)] * 2
        + [jax.ShapeDtypeStruct((16, D), full)],
        grid=(3,),
        in_specs=[whole] * (3 * count + 1),
        out_specs=[part, part, pl.BlockSpec((16, D), lambda c: (0, 0))],
        scratch_shapes=[pltpu.VMEM((count, D, rows), low)],
        compiler_params=pltpu.CompilerParams(vmem_limit_bytes=VMEM_LIMIT),
        cost_estimate=pl.CostEstimate(
            flops=18 * rows * D * D, bytes_accessed=18 << 20, transcendentals=0
        ),
        name="qkv_grads",
    )(*chunks, query_grad, *key_grads, *value_grads)


def two_parts(value, axis, mine):
    keep = lax.dynamic_index_in_dim(value, mine, axis, keepdims=False)
    send = lax.dynamic_index_in_dim(value, 1 - mine, axis, keepdims=False)
    return keep, send.astype(low)


def scatter_dp(parts):
    bits = outer_bits()
    half = len(bits) // 2
    orders = [bits[half * (n % 2) :] + bits[: half * (n % 2)] for n in range(len(parts))]
    me = lax.axis_index("dp")
    yield [send for _, send in parts]
    held = [keep.astype(full) + swap(send, "dp", 1).astype(full) for keep, send in parts]
    held = [
        value.astype(low).reshape(value.shape[:1] + (2,) * len(bits) + value.shape[2:])
        for value in held
    ]
    axes = [list(reversed(bits)) for _ in parts]
    for step in range(len(bits)):
        parts = []
        for n, value in enumerate(held):
            bit = orders[n][step]
            axis = 1 + axes[n].index(bit)
            axes[n].remove(bit)
            parts.append(two_parts(value, axis, (me // bit) % 2))
        yield [send for _, send in parts]
        held = [
            keep.astype(full) + swap(send, "dp", orders[n][step]).astype(full)
            for n, (keep, send) in enumerate(parts)
        ]
        if step < len(bits) - 1:
            held = [value.astype(low) for value in held]
    return held


def scatter_mp(value):
    rank = lax.axis_index("mp")
    for bit in (2, 1):
        pair = value.reshape((2, value.shape[0] // 2) + value.shape[1:])
        keep, send = two_parts(pair, 0, (rank // bit) % 2)
        yield [send]
        value = keep.astype(full) + swap(send, "mp", bit).astype(full)
    return value[0]


def scatter_feed(up_parts, down_parts):
    mp = lax.axis_size("mp")
    up_own, down_own = yield from scatter_dp([up_parts, down_parts])
    block = down_own.shape[1]
    out_own = up_own[mp].reshape(block, mp, -1).transpose(1, 0, 2)
    tall = yield from scatter_mp(jnp.concatenate([up_own[:mp], down_own], axis=1))
    out_grad = yield from scatter_mp(out_own)
    return tall[:block], tall[block:].T, out_grad.T


def scatter_qkv(keep, send):
    rank = lax.axis_index("mp")
    left_part, right_part = yield from scatter_dp(
        [(keep[..., : D // 2], send[..., : D // 2]), (keep[..., D // 2 :], send[..., D // 2 :])]
    )
    upper = rank >= 2
    odd = rank % 2 == 1
    send = jnp.where(upper, left_part, right_part).astype(low)
    yield [send]
    keep = jnp.where(upper, right_part, left_part) + swap(send, "mp", 2).astype(full)
    width = D // lax.axis_size("mp")
    send = jnp.where(odd, keep[..., :width], keep[..., width:]).astype(low)
    yield [send]
    return jnp.where(odd, keep[..., width:], keep[..., :width]) + swap(
        send, "mp", 1
    ).astype(full)


class Steps:
    def __init__(self, steps):
        self.steps = steps
        self.result = None
        self.done = False

    def next(self):
        try:
            return next(self.steps)
        except StopIteration as stop:
            self.result = stop.value
            self.done = True
            return []

    def finish(self):
        while not self.done:
            self.next()
        return self.result


def shards(
    tokens_in,
    timesteps,
    lengths,
    time_table,
    norm_gains,
    norm_biases,
    w_qkv,
    qv_bias,
    w_out,
    out_bias,
    w_up,
    up_bias,
    w_down,
    down_bias,
    cotangent,
    teacher,
):
    rank = lax.axis_index("mp")
    data_rank = lax.axis_index("dp")
    mp = lax.axis_size("mp")
    dp = lax.axis_size("dp")
    own_rows = tokens_in.shape[0]
    length = lax.dynamic_index_in_dim(lengths, data_rank, keepdims=False)
    own_time = lax.dynamic_index_in_dim(timesteps, data_rank, keepdims=False)
    odd = rank % 2 == 1
    upper = rank >= 2
    middle = jnp.logical_or(rank == 1, rank == 2)

    block = w_qkv.shape[1]
    aligned = block % 32 == 0
    narrow = jnp.concatenate([w_qkv.reshape(3 * block, -1), w_out.T])
    first_swap = swap(narrow, "mp", 1)
    pair = jnp.concatenate(
        [jnp.where(odd, first_swap, narrow), jnp.where(odd, narrow, first_swap)], axis=1
    )
    second_swap = swap(pair, "mp", 2)
    wide = jnp.concatenate(
        [jnp.where(upper, second_swap, pair), jnp.where(upper, pair, second_swap)], axis=1
    )
    qkv_rows, out_rows = wide[: 3 * block], wide[3 * block :]
    up_swap = swap(after(w_up, first_swap), "mp", 1)

    table_row = lax.dynamic_slice_in_dim(time_table, own_time, 1).astype(full)
    start_state = tokens_in.astype(full) + table_row
    unit_one, inverse_one = norm_stats(start_state)
    first_norm = (unit_one * norm_gains[0] + norm_biases[0]).astype(low)
    sent = after(first_norm, second_swap)
    along = lambda value, pairs: lax.ppermute(value, "mp", pairs)
    from_left = along(sent, [(0, 1), (1, 2), (2, 3)])
    from_right = along(sent, [(1, 0), (2, 1), (3, 2)])
    near = jnp.where(rank == 0, from_right, from_left)

    up_pair = jnp.concatenate([w_up, up_swap])
    up_other = swap(after(up_pair, second_swap), "mp", 2)
    down_own = w_down.T
    down_swap = swap(after(down_own, second_swap), "mp", 1)
    down_pair = jnp.concatenate([down_own, down_swap])
    down_other = swap(after(down_pair, up_other), "mp", 2)

    if aligned:
        split = 3 * block // 2
        gathered = gather_dp([qkv_rows[:split], qkv_rows[split:]])
        arrived = [array for pieces in gathered for _, array in pieces]
        arrays, plan = plan_of(
            gathered,
            [
                [(0, block, 0, 0, 0, 0), (block, split - block, 0, 0, 0, D)],
                [
                    (0, 2 * block - split, 0, 0, 0, D + split - block),
                    (2 * block - split, block, 0, 0, 0, 2 * D),
                ],
            ],
        )
        (qkv_weight,) = place(arrays, plan, block, [(3 * D, D)])
        qkv_weight = qkv_weight.reshape(3, D, D)
        early = [gathered[0][0][1], gathered[1][0][1]]
        ups = gather_dp([up_pair, up_other], early)
        lates = [ups[0][0][1], ups[1][0][1]]
        downs = gather_dp(
            [
                jnp.concatenate([down_pair, out_rows[: block // 2]]),
                jnp.concatenate([down_other, out_rows[block // 2 :]]),
            ],
            lates,
        )
        up_arrays, up_plan = plan_of(
            ups,
            [
                [(0, block, 0, 0, D, 0), (block, block, 0, 1, D, 0)],
                [(0, block, 0, 2, D, 0), (block, block, 0, 3, D, 0)],
            ],
        )
        down_arrays, down_plan = plan_of(
            downs,
            [
                [
                    (0, block, 1, 0, D, 0),
                    (block, block, 1, 1, D, 0),
                    (2 * block, block // 2, 2, 0, 0, 0),
                ],
                [
                    (0, block, 1, 2, D, 0),
                    (block, block, 1, 3, D, 0),
                    (2 * block, block // 2, 2, 0, 0, block // 2),
                ],
            ],
        )
        arrays, plan = up_arrays + down_arrays, up_plan + down_plan
    else:
        early = []
        qkv_weight = lax.all_gather(
            qkv_rows.reshape(3, block, D), "dp", axis=1, tiled=True
        )
        arrays = [
            lax.all_gather(w_up, ("mp", "dp"), axis=0, tiled=True),
            lax.all_gather(down_own, ("mp", "dp"), axis=0, tiled=True),
            lax.all_gather(out_rows, "dp", axis=0, tiled=True),
        ]
        plan = [[(0, array.shape[0], n, None, 0, 0, 0)] for n, array in enumerate(arrays)]

    queries = dot_of(first_norm, qkv_weight[0], 1, 0) + qv_bias[0]
    queries = (queries.astype(low) * score_scale).astype(low)
    hop_right = after(from_left, *early)
    hop_left = after(from_right, *early)
    second = jnp.where(
        upper,
        along(hop_right, [(1, 2), (2, 3)]),
        along(hop_left, [(1, 0), (2, 1)]),
    )
    indices = [
        rank,
        jnp.where(rank == 0, 1, rank - 1),
        jnp.where(upper, rank - 2, rank + 2),
        jnp.where(middle, rank + 1, 3 - rank),
    ]
    scalars = [jnp.stack([index, length]).astype(jnp.int32) for index in indices]

    def project(chunk):
        return (
            dot_of(chunk, qkv_weight[1], 1, 0).astype(low),
            (dot_of(chunk, qkv_weight[2], 1, 0) + qv_bias[1]).astype(low),
        )

    keys, values = map(list, zip(*[project(first_norm), project(near)]))
    state = attend_forward(
        after(queries, hop_right, hop_left),
        keys,
        values,
        jnp.stack(indices[:2] + [length]),
        None,
    )
    second = after(second, state[0])
    last = jnp.where(middle, from_right, along(second, [(1, 0), (2, 3)]))
    chunks = [first_norm, near, second, last]
    for chunk in chunks[2:]:
        key, value = project(chunk)
        keys.append(key)
        values.append(value)
    mixed, logs = attend_forward(
        queries, keys[2:], values[2:], jnp.stack(indices[2:] + [length]), state
    )

    loss_weight = lengths.shape[0] * MAXLEN / jnp.sum(lengths).astype(full)
    vectors = jnp.concatenate(
        [
            table_row,
            out_bias[None],
            norm_gains[1:2],
            norm_biases[1:2],
            down_bias[None],
            jnp.full((3, D), loss_weight),
            up_bias.reshape(-1, D),
            jnp.zeros((4, D), full),
        ]
    )
    limit = (length - rank * own_rows).reshape(1)
    (
        output,
        final_low,
        hidden_act,
        pre_grad,
        second_norm,
        middle_low,
        attended,
        middle_grad,
        attended_grad,
        deltas,
        log_rows,
        sums,
    ) = middle_call(
        limit, vectors, tokens_in, mixed, logs, cotangent, teacher, arrays, plan, block
    )
    gain_two, shift_two, middle_sum, final_sum = sums[0], sums[1], sums[2], sums[3]
    down_keep, down_send, up_keep, up_send = feed_grads(
        final_low, hidden_act, second_norm, pre_grad, middle_low, attended, dp
    )

    feed = Steps(scatter_feed((up_keep, up_send), (down_keep, down_send)))
    key_grads = [None] * 4
    value_grads = [None] * 4
    firsts = [None] * 4
    query_grad = None
    for n in (3, 2, 1, 0):
        waits = feed.next()
        if n == 1:
            waits = waits + [payload]
        query_grad, key_grads[n], value_grads[n], firsts[n] = attend_backward(
            queries,
            keys[n],
            values[n],
            after(attended_grad, *waits),
            log_rows,
            deltas,
            qkv_weight,
            scalars[n],
            query_grad,
            n == 0,
        )
        if n == 3:
            back_last = along(firsts[3], [(0, 1), (3, 2)]).astype(full)
        elif n == 2:
            payload = (firsts[2] + back_last).astype(low)
            back_right = along(payload, [(0, 1), (1, 2)]).astype(full)
            back_left = along(payload, [(3, 2), (2, 1)]).astype(full)
        elif n == 1:
            to_right = jnp.where(
                rank == 0, firsts[1], firsts[3].astype(full) + back_right
            ).astype(low)
            to_left = (firsts[1] + back_left).astype(low)
            final_right = along(to_right, [(0, 1), (1, 2), (2, 3)])
            final_left = along(to_left, [(3, 2), (2, 1), (1, 0)])
    first_grad = firsts[0] + final_right.astype(full) + final_left.astype(full)
    qkv_keep, qkv_send, bias_sums = qkv_grads(chunks, query_grad, key_grads, value_grads, dp)
    qv_bias_part = jnp.stack([bias_sums[0], bias_sums[8]])
    qkv_grad = Steps(scatter_qkv(qkv_keep, qkv_send)).finish()
    up_grad, down_grad, out_grad = feed.finish()

    start_part, gain_one, shift_one = norm_back(
        unit_one, inverse_one, norm_gains[0], first_grad
    )
    input_grad = middle_grad + start_part
    sequence_sum = jnp.sum(input_grad, axis=0)
    own_slot = (jnp.arange(dp) == data_rank).astype(full)
    total = jnp.concatenate(
        [
            jnp.stack([gain_one, gain_two, shift_one, shift_two]),
            qv_bias_part,
            jnp.stack([middle_sum, final_sum]),
            sums[8 : 8 + FF // D],
            own_slot[:, None] * sequence_sum[None, :],
        ]
    )
    for bit in [1] + outer_bits():
        total = total + swap(total, "dp", bit)
    for bit in (1, 2):
        total = total + swap(total, "mp", bit)
    fixed = 8 + FF // D
    chosen = (timesteps[None, :] == jnp.arange(time_table.shape[0])[:, None]).astype(full)
    table_grad = lax.dot_general(
        chosen,
        total[fixed:],
        (((1,), (0,)), ((), ())),
        precision=lax.Precision.HIGHEST,
        preferred_element_type=full,
    )
    return (
        output,
        input_grad,
        table_grad,
        total[0:2],
        total[2:4],
        qkv_grad,
        total[4:6],
        out_grad,
        total[6],
        up_grad,
        total[8:fixed].reshape(FF),
        down_grad,
        total[7],
    )


def solution(mesh):
    rows = P(both, None)
    placed = (
        rows,
        P(),
        P(),
        P(),
        P(),
        P(),
        P(None, "dp", "mp"),
        P(),
        P("mp", "dp"),
        P(),
        P("dp", "mp"),
        P(),
        P("mp", "dp"),
        P(),
        rows,
        rows,
    )
    return jax.shard_map(
        shards,
        mesh=mesh,
        in_specs=placed,
        out_specs=(
            rows,
            rows,
            P(),
            P(),
            P(),
            P(None, "dp", "mp"),
            P(),
            P("mp", "dp"),
            P(),
            P("dp", "mp"),
            P(),
            P("mp", "dp"),
            P(),
        ),
        check_vma=False,
    )
```

time: 927 us -> 468 us (0.50)
  Pallas kernels: 549 us -> 150 us
  matrix products: 57.8 us -> 19.6 us
  waiting for transfers between devices: 175 us -> 145 us
  other arithmetic: 28.7 us -> 43.3 us
    pallas_call x6, Pallas kernels: 504 us -> 85.5 us  [the longest x2 30.2 us: attend_forward(): pl.pallas_call(functools.partial(forward_kernel, first), out_shape=(wide,...]
    ppermute x10, waiting for transfers between devices: 56 us -> 7.32 us  [shards(): along = lambda value, pairs: lax.ppermute(value, 'mp', pairs)]
    dot_general x6 -> x0, matrix products: 23.7 us -> none  [the longest x1 4.72 us: shards(): jnp.einsum('td,mtf->mdf', second_norm, pre_grad, preferred_element_type=f...]
    pallas_call x4, Pallas kernels: 44.8 us -> 64.7 us  [attend_backward(): pl.pallas_call(functools.partial(backward_kernel, first, last), out_shape...]
    ppermute x43 -> x53, waiting for transfers between devices: 119 us -> 138 us  [swap(): return lax.ppermute(value, axis, [(i, i ^ bit) for i in range(count)])]
    dot_general x24 -> x9, matrix products: 31.2 us -> 16.6 us  [dot_of(): lax.dot_general(left_side, right_side, (((left_dim,), (right_dim,)), ((),...]
    convert_element_type x3 -> x7, other arithmetic: 1.17 us -> 14.4 us  [the longest x3 8.64 us: scatter_dp(): value.astype(low)]
    ppermute x43 -> x53, starting transfers between devices: 45.4 us -> 44.2 us  [swap(): return lax.ppermute(value, axis, [(i, i ^ bit) for i in range(count)])]
  transfers between devices with their start and end apart: 53 -> 63, of which waited for: 19 -> 20; matrix products, arithmetic and copies ran while one was open for 6% -> 16% of each run, Pallas kernels for 20% -> 24%
where the time goes in v3:
time: 468 us; the launch traced here: 459 us
  Pallas kernels  150 us (32%)
  waiting for transfers between devices  145 us (31%)
  starting transfers between devices  70.8 us (15%)
  other arithmetic  43.3 us (9%)
  local copies, waits for them, and re-layouts  24.7 us (5%)
  matrix products  19.6 us (4%)
  between operations  5.4 us (1%)
    ppermute x53, waiting for transfers between devices, swap(): return lax.ppermute(value, axis, [(i, i ^ bit) for i in range(count)])  138 us
    pallas_call x4, Pallas kernels, attend_backward(): pl.pallas_call(functools.partial(backward_kernel, first, last), out_shape...  64.7 us
    ppermute x53, starting transfers between devices, swap(): return lax.ppermute(value, axis, [(i, i ^ bit) for i in range(count)])  44.2 us
    pallas_call x2, Pallas kernels, attend_forward(): pl.pallas_call(functools.partial(forward_kernel, first), out_shape=(wide,...  30.2 us
    pallas_call x1, Pallas kernels, middle_call(): pl.pallas_call(functools.partial(middle_kernel, plan, block, len(arrays))...  27.3 us
    ppermute x10, starting transfers between devices, shards(): along = lambda value, pairs: lax.ppermute(value, 'mp', pairs)  26.6 us
    dot_general x9, matrix products, dot_of(): lax.dot_general(left_side, right_side, (((left_dim,), (right_dim,)), ((),...  16.6 us
    pallas_call x1, Pallas kernels, feed_grads(): pl.pallas_call(feed_grad_kernel, out_shape=[jax.ShapeDtypeStruct(shape, l...  12.2 us
  transfers between devices with their start and end apart: 63, of which 20 were waited for; matrix products, arithmetic and copies ran while one was open for 16% of the time, Pallas kernels for 24%

profile of v3, /device:TPU:0, one launch (start us, length us, event | category | flops | bytes accessed | tf_op | source)
XLA Modules:
  0.0 458.9 jit_solution(7077943435396068235)
XLA Ops:
  22.4 7.5 %collective-permute-done.1 = bf16[384,384]{1,0:T(8,128)(2,1)S(1)} collective-permute-done((bf16[384,384]{1,0:T(8,128)(2,1)S(1)}, bf16[384,384]{1,0:T(8,128)(2,1)S(1)}, u32[]{:S(2)}, u32[]{:S(2)}) %collective-permute-start.1) | collective-permute-done | bytes 294944 | tf_op jit(solution)/shard_map/ppermute | solution.py:264
  34.6 4.6 %collective-permute-start.10 = (bf16[512,768]{1,0:T(8,128)(2,1)S(1)}, bf16[512,768]{1,0:T(8,128)(2,1)}, u32[]{:S(2)}, u32[]{:S(2)}) collective-permute-start(bf16[512,768]{1,0:T(8,128)(2,1)S(1)} %add_convert_fusion.11.refs_0_), channel_id=1, source_target_pairs={{0,1},{1,2},{2,3},{4,5},{5,6},{6,7},{8,9},{9,10},{10,11},{12,13},{... | collective-permute-start | bytes 2359304 | tf_op jit(solution)/shard_map/ppermute | solution.py:864
  44.0 5.6 %collective-permute-done.20 = bf16[192,768]{1,0:T(8,128)(2,1)S(1)} collective-permute-done((bf16[192,768]{1,0:T(8,128)(2,1)S(1)}, bf16[192,768]{1,0:T(8,128)(2,1)S(1)}, u32[]{:S(2)}, u32[]{:S(2)}) %collective-permute-start.20) | collective-permute-done | bytes 294944 | tf_op jit(solution)/shard_map/ppermute | solution.py:264
  51.1 17.1 %collective-permute-done.25 = bf16[96,768]{1,0:T(8,128)(2,1)S(1)} collective-permute-done((bf16[96,768]{1,0:T(8,128)(2,1)S(1)}, bf16[96,768]{1,0:T(8,128)(2,1)S(1)}, u32[]{:S(2)}, u32[]{:S(2)}) %collective-permute-start.25) | collective-permute-done | bytes 147488 | tf_op jit(solution)/shard_map/ppermute | solution.py:264
  71.9 12.4 %collective-permute-done.30 = bf16[192,768]{1,0:T(8,128)(2,1)S(1)} collective-permute-done((bf16[192,768]{1,0:T(8,128)(2,1)S(1)}, bf16[192,768]{1,0:T(8,128)(2,1)S(1)}, u32[]{:S(2)}, u32[]{:S(2)}) %collective-permute-start.30) | collective-permute-done | bytes 294944 | tf_op jit(solution)/shard_map/ppermute | solution.py:264
  106.5 14.8 %attend_forward.2 = (f32[512,768]{1,0:T(8,128)}, f32[512,768]{1,0:T(8,128)}, f32[512,768]{1,0:T(8,128)}) custom-call(s32[3]{0:T(128)} %add_add_fusion.1.scalars, bf16[512,768]{1,0:T(8,128)(2,1)} %fusion.5.q_ref, bf16[512,768]{1,0:T(8,128)(2,1)} %convolution_convert_fusion.3.refs_0_.k_ref, bf16[512,768]{1,0:T(8,128)(2,1)} %convolution_convert_fusion.2.refs_1_.k_ref, ...), custom_call_target="tpu_custom_call" | custom-call | flops 6442450944 | bytes 9437184 | tf_op jit(solution)/shard_map/attend_forward/pallas_call | solution.py:112
  126.2 6.6 %collective-permute-done.26 = bf16[240,768]{1,0:T(8,128)(2,1)S(1)} collective-permute-done((bf16[240,768]{1,0:T(8,128)(2,1)S(1)}, bf16[240,768]{1,0:T(8,128)(2,1)S(1)}, u32[]{:S(2)}, u32[]{:S(2)}) %collective-permute-start.26) | collective-permute-done | bytes 368672 | tf_op jit(solution)/shard_map/ppermute | solution.py:264
  139.0 7.3 %collective-permute-done.14 = bf16[512,768]{1,0:T(8,128)(2,1)S(1)} collective-permute-done((bf16[512,768]{1,0:T(8,128)(2,1)S(1)}, bf16[512,768]{1,0:T(8,128)(2,1)S(1)}, u32[]{:S(2)}, u32[]{:S(2)}) %collective-permute-start.14) | collective-permute-done | bytes 786464 | tf_op jit(solution)/shard_map/ppermute | solution.py:864
  148.5 11.9 %collective-permute-done.32.refs_20_ = bf16[480,768]{1,0:T(8,128)(2,1)S(1)} collective-permute-done((bf16[480,768]{1,0:T(8,128)(2,1)S(1)}, bf16[480,768]{1,0:T(8,128)(2,1)S(1)}, u32[]{:S(2)}, u32[]{:S(2)}) %collective-permute-start.32) | collective-permute-done | bytes 737312 | tf_op jit(solution)/shard_map/ppermute | solution.py:264
  164.1 15.4 %attend_forward.3 = (f32[512,768]{1,0:T(8,128)}, f32[512,768]{1,0:T(8,128)}) custom-call(s32[3]{0:T(128)} %add_add_fusion.scalars, bf16[512,768]{1,0:T(8,128)(2,1)} %fusion.5.q_ref, bf16[512,768]{1,0:T(8,128)(2,1)} %convolution_convert_fusion.1.refs_0_.k_ref, bf16[512,768]{1,0:T(8,128)(2,1)} %convolution_convert_fusion.refs_1_.k_ref, ...), custom_call_target="tpu_custom_call" | custom-call | flops 6442450944 | bytes 9437184 | tf_op jit(solution)/shard_map/attend_forward/pallas_call | solution.py:112
  180.8 27.3 %middle.1 = (bf16[512,768]{1,0:T(8,128)(2,1)}, bf16[512,768]{1,0:T(8,128)(2,1)}, bf16[4,512,768]{2,1,0:T(8,128)(2,1)}, bf16[4,512,768]{2,1,0:T(8,128)(2,1)}, bf1...) custom-call(s32[1]{0:T(128)} %bitcast.1.refs_0_, ...), custom_call_target="tpu_custom_call" | custom-call | flops 24159191040 | bytes 31457280 | tf_op jit(solution)/shard_map/middle/pallas_call | solution.py:548
  208.1 12.2 %feed_grads.1 = (bf16[4,4,96,768]{3,2,1,0:T(8,128)(2,1)}, bf16[4,4,96,768]{3,2,1,0:T(8,128)(2,1)}, bf16[5,4,96,768]{3,2,1,0:T(8,128)(2,1)}, bf16[5,4,96,768]{3,2,1,0:T(8,128)(2,1)}) custom-call(bf16[512,768]{1,0:T(8,128)(2,1)} %get-tuple-element.91.final_ref, bf16[4,512,768]{2,1,0:T(8,128)(2,1)} %get-tuple-element.92.act_ref, ...), custom_call_target="tpu_custom_call" | custom-call | flops 12079595520 | bytes 20971520 | tf_op jit(solution)/shard_map/feed_grads/pallas_call | solution.py:640
  232.0 15.3 %attend_backward.4 = (f32[512,768]{1,0:T(8,128)}, bf16[512,768]{1,0:T(8,128)(2,1)}, bf16[512,768]{1,0:T(8,128)(2,1)}, bf16[512,768]{1,0:T(8,128)(2,1)}) custom-call(s32[2]{0:T(128)} %pad_add_fusion.3.scalars, bf16[512,768]{1,0:T(8,128)(2,1)} %fusion.5.q_ref, bf16[512,768]{1,0:T(8,128)(2,1)} %convolution_convert_fusion.refs_1_.k_ref, ...), custom_call_target="tpu_custom_call" | custom-call | flops 8053063680 | bytes 6291456 | tf_op jit(solution)/shard_map/attend_backward/pallas_call | solution.py:222
  247.3 5.9 %collective-permute-start.41 = (bf16[512,768]{1,0:T(8,128)(2,1)}, bf16[512,768]{1,0:T(8,128)(2,1)}, u32[]{:S(2)}, u32[]{:S(2)}) collective-permute-start(bf16[512,768]{1,0:T(8,128)(2,1)} %get-tuple-element.108), channel_id=1, source_target_pairs={{0,1},{3,2},{4,5},{7,6},{8,9},{11,10},{12,13},{15,14},{16,17},{19,... | collective-permute-start | bytes 2359304 | tf_op jit(solution)/shard_map/ppermute | solution.py:864
  263.4 15.5 %attend_backward.5 = (f32[512,768]{1,0:T(8,128)}, bf16[512,768]{1,0:T(8,128)(2,1)}, bf16[512,768]{1,0:T(8,128)(2,1)}, f32[512,768]{1,0:T(8,128)}) custom-call(s32[2]{0:T(128)} %pad_add_fusion.2.scalars, bf16[512,768]{1,0:T(8,128)(2,1)} %fusion.5.q_ref, bf16[512,768]{1,0:T(8,128)(2,1)} %convolution_convert_fusion.1.refs_0_.k_ref, ...), custom_call_target="tpu_custom_call" | custom-call | flops 8053063680 | bytes 6291456 | tf_op jit(solution)/shard_map/attend_backward/pallas_call | solution.py:222
  281.6 5.5 %collective-permute-start.42 = (bf16[512,768]{1,0:T(8,128)(2,1)}, bf16[512,768]{1,0:T(8,128)(2,1)}, u32[]{:S(2)}, u32[]{:S(2)}) collective-permute-start(bf16[512,768]{1,0:T(8,128)(2,1)} %add_convert_fusion.5), channel_id=1, source_target_pairs={{0,1},{1,2},{4,5},{5,6},{8,9},{9,10},{12,13},{13,14},{16,17},{17,1... | collective-permute-start | bytes 2359304 | tf_op jit(solution)/shard_map/ppermute | solution.py:864
  288.6 17.7 %collective-permute-done.40 = bf16[4,96,768]{2,1,0:T(8,128)(2,1)S(1)} collective-permute-done((bf16[4,96,768]{2,1,0:T(8,128)(2,1)S(1)}, bf16[4,96,768]{2,1,0:T(8,128)(2,1)S(1)}, u32[]{:S(2)}, u32[]{:S(2)}) %collective-permute-start.40) | collective-permute-done | bytes 589856 | tf_op jit(solution)/shard_map/ppermute | solution.py:264
  311.0 15.8 %attend_backward.6 = (f32[512,768]{1,0:T(8,128)}, bf16[512,768]{1,0:T(8,128)(2,1)}, bf16[512,768]{1,0:T(8,128)(2,1)}, f32[512,768]{1,0:T(8,128)}) custom-call(s32[2]{0:T(128)} %pad_add_fusion.1.scalars, bf16[512,768]{1,0:T(8,128)(2,1)} %fusion.5.q_ref, bf16[512,768]{1,0:T(8,128)(2,1)} %convolution_convert_fusion.2.refs_1_.k_ref, ...), custom_call_target="tpu_custom_call" | custom-call | flops 8053063680 | bytes 6291456 | tf_op jit(solution)/shard_map/attend_backward/pallas_call | solution.py:222
  338.0 18.1 %attend_backward.7 = (bf16[512,768]{1,0:T(8,128)(2,1)}, bf16[512,768]{1,0:T(8,128)(2,1)}, bf16[512,768]{1,0:T(8,128)(2,1)}, f32[512,768]{1,0:T(8,128)}) custom-call(s32[2]{0:T(128)} %pad_add_fusion.scalars, bf16[512,768]{1,0:T(8,128)(2,1)} %fusion.5.q_ref, bf16[512,768]{1,0:T(8,128)(2,1)} %convolution_convert_fusion.3.refs_0_.k_ref, ...), custom_call_target="tpu_custom_call" | custom-call | flops 8053063680 | bytes 6291456 | tf_op jit(solution)/shard_map/attend_backward/pallas_call | solution.py:222
  356.3 11.7 %qkv_grads.1 = (bf16[3,4,96,768]{3,2,1,0:T(8,128)(2,1)}, bf16[3,4,96,768]{3,2,1,0:T(8,128)(2,1)}, f32[16,768]{1,0:T(8,128)}) custom-call(bf16[512,768]{1,0:T(8,128)(2,1)} %copy-done.13, bf16[512,768]{1,0:T(8,128)(2,1)} %copy-done.10, bf16[512,768]{1,0:T(8,128)(2,1)} %copy-done.11, bf16[512,768]{1,0:T(8,128)(2,1)} %copy-done.12, ...), custom_call_target="tpu_custom_call" | custom-call | flops 5435817984 | bytes 18874368 | tf_op jit(solution)/shard_map/qkv_grads/pallas_call | solution.py:707
  392.8 25.8 %collective-permute-done.50 = f32[20,768]{1,0:T(8,128)S(1)} collective-permute-done((f32[20,768]{1,0:T(8,128)S(1)}, f32[20,768]{1,0:T(8,128)S(1)}, u32[]{:S(2)}, u32[]{:S(2)}) %collective-permute-start.50) | collective-permute-done | bytes 61472 | tf_op jit(solution)/shard_map/ppermute | solution.py:264
  425.8 9.0 %collective-permute-done.55 = bf16[3,2,96,384]{3,2,0,1:T(8,128)(2,1)S(1)} collective-permute-done((bf16[3,2,96,384]{3,2,0,1:T(8,128)(2,1)S(1)}, bf16[3,2,96,384]{3,2,0,1:T(8,128)(2,1)S(1)}, u32[]{:S(2)}, u32[]{:S(2)}) %collective-permute-start.55) | collective-permute-done | bytes 442400 | tf_op jit(solution)/shard_map/ppermute | solution.py:264
  443.2 4.4 collective-permute-done.62
  453.6 4.3 collective-permute-done.58
  (335 shorter events, 161.9 us)
Async XLA Ops:
  34.6 52.5 %collective-permute-start.10 = (bf16[512,768]{1,0:T(8,128)(2,1)S(1)}, bf16[512,768]{1,0:T(8,128)(2,1)}, u32[]{:S(2)}, u32[]{:S(2)}) collective-permute-start(bf16[512,768]{1,0:T(8,128)(2,1)S(1)} %add_convert_fusion.11.refs_0_), channel_id=1, source_target_pairs={{0,1},{1,2},{2,3},{4,5},{5,6},{6,7},{8,9},{9,10},{10,11},{12,13},{... | collective-permute-start | bytes 2359304 | tf_op jit(solution)/shard_map/ppermute | solution.py:864
  39.3 45.8 %collective-permute-start.12 = (bf16[512,768]{1,0:T(8,128)(2,1)S(1)}, bf16[512,768]{1,0:T(8,128)(2,1)S(1)}, u32[]{:S(2)}, u32[]{:S(2)}) collective-permute-start(bf16[512,768]{1,0:T(8,128)(2,1)S(1)} %add_convert_fusion.11.refs_0_), channel_id=1, source_target_pairs={{1,0},{2,1},{3,2},{5,4},{6,5},{7,6},{9,8},{10,9},{11,10},{13,12},{... | collective-permute-start | bytes 2359304 | tf_op jit(solution)/shard_map/ppermute | solution.py:864
  40.6 27.6 %collective-permute-start.25 = (bf16[96,768]{1,0:T(8,128)(2,1)S(1)}, bf16[96,768]{1,0:T(8,128)(2,1)S(1)}, u32[]{:S(2)}, u32[]{:S(2)}) collective-permute-start(bf16[96,768]{1,0:T(8,128)(2,1)S(1)} %bitcast.119), channel_id=1, source_target_pairs={{0,1},{1,0},{2,3},{3,2},{4,5},{5,4},{6,7},{7,6},{8,9},{9,8},{10,11... | collective-permute-start | bytes 442376 | tf_op jit(solution)/shard_map/ppermute | solution.py:264
  43.4 26.1 %collective-permute-start.16 = (bf16[192,768]{1,0:T(8,128)(2,1)S(1)}, bf16[192,768]{1,0:T(8,128)(2,1)S(1)}, u32[]{:S(2)}, u32[]{:S(2)}) collective-permute-start(bf16[192,768]{1,0:T(8,128)(2,1)S(1)} %constant_dynamic-update-slice_fusion), channel_id=1, source_target_pairs={{0,8},{4,12},{8,0},{12,4},{16,24},{20,28},{24,16},{28,20},{1,9},{5... | collective-permute-start | bytes 884744 | tf_op jit(solution)/shard_map/ppermute | solution.py:264
  87.1 49.6 %collective-permute-start.17 = (bf16[384,768]{1,0:T(8,128)(2,1)}, bf16[384,768]{1,0:T(8,128)(2,1)}, u32[]{:S(2)}, u32[]{:S(2)}) collective-permute-start(bf16[384,768]{1,0:T(8,128)(2,1)} %constant_dynamic-update-slice_fusion.2.refs_7_), channel_id=1, source_target_pairs={{0,16},{4,20},{8,24},{12,28},{16,0},{20,4},{24,8},{28,12},{1,17},{... | collective-permute-start | bytes 1769480 | tf_op jit(solution)/shard_map/ppermute | solution.py:264
  87.7 51.2 %collective-permute-start.18 = (bf16[384,768]{1,0:T(8,128)(2,1)}, bf16[384,768]{1,0:T(8,128)(2,1)}, u32[]{:S(2)}, u32[]{:S(2)}) collective-permute-start(bf16[384,768]{1,0:T(8,128)(2,1)} %constant_dynamic-update-slice_fusion.2.refs_7_), channel_id=1, source_target_pairs={{0,4},{4,0},{8,12},{12,8},{16,20},{20,16},{24,28},{28,24},{1,5},{5... | collective-permute-start | bytes 1769480 | tf_op jit(solution)/shard_map/ppermute | solution.py:264
  87.8 36.8 %collective-permute-start.31 = (bf16[240,768]{1,0:T(8,128)(2,1)S(1)}, bf16[240,768]{1,0:T(8,128)(2,1)S(1)}, u32[]{:S(2)}, u32[]{:S(2)}) collective-permute-start(bf16[240,768]{1,0:T(8,128)(2,1)S(1)} %fusion.22), channel_id=1, source_target_pairs={{0,16},{4,20},{8,24},{12,28},{16,0},{20,4},{24,8},{28,12},{1,17},{... | collective-permute-start | bytes 1105928 | tf_op jit(solution)/shard_map/ppermute | solution.py:264
  89.5 31.8 %collective-permute-start.13 = (bf16[512,768]{1,0:T(8,128)(2,1)S(1)}, bf16[512,768]{1,0:T(8,128)(2,1)}, u32[]{:S(2)}, u32[]{:S(2)}) collective-permute-start(bf16[512,768]{1,0:T(8,128)(2,1)S(1)} %collective-permute-done.12), channel_id=1, source_target_pairs={{1,0},{2,1},{5,4},{6,5},{9,8},{10,9},{13,12},{14,13},{17,16},{18,1... | collective-permute-start | bytes 2359304 | tf_op jit(solution)/shard_map/ppermute | solution.py:864
  90.8 32.1 %collective-permute-start.11 = (bf16[512,768]{1,0:T(8,128)(2,1)}, bf16[512,768]{1,0:T(8,128)(2,1)}, u32[]{:S(2)}, u32[]{:S(2)}) collective-permute-start(bf16[512,768]{1,0:T(8,128)(2,1)} %collective-permute-done.10), channel_id=1, source_target_pairs={{1,2},{2,3},{5,6},{6,7},{9,10},{10,11},{13,14},{14,15},{17,18},{18... | collective-permute-start | bytes 2359304 | tf_op jit(solution)/shard_map/ppermute | solution.py:864
  132.8 27.6 %collective-permute-start.32 = (bf16[480,768]{1,0:T(8,128)(2,1)S(1)}, bf16[480,768]{1,0:T(8,128)(2,1)S(1)}, u32[]{:S(2)}, u32[]{:S(2)}) collective-permute-start(bf16[480,768]{1,0:T(8,128)(2,1)S(1)} %constant_dynamic-update-slice_fusion.8.refs_19_), channel_id=1, source_target_pairs={{0,8},{4,12},{8,0},{12,4},{16,24},{20,28},{24,16},{28,20},{1,9},{5... | collective-permute-start | bytes 2211848 | tf_op jit(solution)/shard_map/ppermute | solution.py:264
  148.0 31.5 %collective-permute-start.28 = (bf16[480,768]{1,0:T(8,128)(2,1)}, bf16[480,768]{1,0:T(8,128)(2,1)S(1)}, u32[]{:S(2)}, u32[]{:S(2)}) collective-permute-start(bf16[480,768]{1,0:T(8,128)(2,1)} %constant_dynamic-update-slice_fusion.6.refs_15_), channel_id=1, source_target_pairs={{0,4},{4,0},{8,12},{12,8},{16,20},{20,16},{24,28},{28,24},{1,5},{5... | collective-permute-start | bytes 2211848 | tf_op jit(solution)/shard_map/ppermute | solution.py:264
  220.4 32.8 %collective-permute-start.35 = (bf16[5,4,96,768]{3,2,1,0:T(8,128)(2,1)}, bf16[5,4,96,768]{3,2,1,0:T(8,128)(2,1)S(1)}, u32[]{:S(2)}, u32[]{:S(2)}) collective-permute-start(bf16[5,4,96,768]{3,2,1,0:T(8,128)(2,1)} %get-tuple-element.98), channel_id=1, source_target_pairs={{0,4},{4,0},{8,12},{12,8},{16,20},{20,16},{24,28},{28,24},{1,5},{5... | collective-permute-start | bytes 8847368 | tf_op jit(solution)/shard_map/ppermute | solution.py:264
  231.5 29.7 %collective-permute-start.39 = (bf16[4,2,96,768]{3,2,0,1:T(8,128)(2,1)}, bf16[4,2,96,768]{3,2,0,1:T(8,128)(2,1)}, u32[]{:S(2)}, u32[]{:S(2)}) collective-permute-start(bf16[4,2,96,768]{3,2,0,1:T(8,128)(2,1)} %bitcast.96), channel_id=1, source_target_pairs={{0,16},{4,20},{8,24},{12,28},{16,0},{20,4},{24,8},{28,12},{1,17},{... | collective-permute-start | bytes 3538952 | tf_op jit(solution)/shard_map/ppermute | solution.py:264
  247.3 31.6 %collective-permute-start.41 = (bf16[512,768]{1,0:T(8,128)(2,1)}, bf16[512,768]{1,0:T(8,128)(2,1)}, u32[]{:S(2)}, u32[]{:S(2)}) collective-permute-start(bf16[512,768]{1,0:T(8,128)(2,1)} %get-tuple-element.108), channel_id=1, source_target_pairs={{0,1},{3,2},{4,5},{7,6},{8,9},{11,10},{12,13},{15,14},{16,17},{19,... | collective-permute-start | bytes 2359304 | tf_op jit(solution)/shard_map/ppermute | solution.py:864
  259.7 47.9 %collective-permute-start.36 = (bf16[5,2,96,768]{3,2,1,0:T(8,128)(2,1)}, bf16[5,2,96,768]{3,2,1,0:T(8,128)(2,1)}, u32[]{:S(2)}, u32[]{:S(2)}) collective-permute-start(bf16[5,2,96,768]{3,2,1,0:T(8,128)(2,1)} %dynamic-slice_bitcast_fusion), channel_id=1, source_target_pairs={{0,8},{4,12},{8,0},{12,4},{16,24},{20,28},{24,16},{28,20},{1,9},{5... | collective-permute-start | bytes 4423688 | tf_op jit(solution)/shard_map/ppermute | solution.py:264
  262.8 43.5 %collective-permute-start.40 = (bf16[4,96,768]{2,1,0:T(8,128)(2,1)S(1)}, bf16[4,96,768]{2,1,0:T(8,128)(2,1)S(1)}, u32[]{:S(2)}, u32[]{:S(2)}) collective-permute-start(bf16[4,96,768]{2,1,0:T(8,128)(2,1)S(1)} %dynamic-slice_bitcast_fusion.2), channel_id=1, source_target_pairs={{0,8},{4,12},{8,0},{12,4},{16,24},{20,28},{24,16},{28,20},{1,9},{5... | collective-permute-start | bytes 1769480 | tf_op jit(solution)/shard_map/ppermute | solution.py:264
  281.6 45.2 %collective-permute-start.42 = (bf16[512,768]{1,0:T(8,128)(2,1)}, bf16[512,768]{1,0:T(8,128)(2,1)}, u32[]{:S(2)}, u32[]{:S(2)}) collective-permute-start(bf16[512,768]{1,0:T(8,128)(2,1)} %add_convert_fusion.5), channel_id=1, source_target_pairs={{0,1},{1,2},{4,5},{5,6},{8,9},{9,10},{12,13},{13,14},{16,17},{17,1... | collective-permute-start | bytes 2359304 | tf_op jit(solution)/shard_map/ppermute | solution.py:864
  287.0 44.8 %collective-permute-start.44 = (bf16[512,768]{1,0:T(8,128)(2,1)}, bf16[512,768]{1,0:T(8,128)(2,1)}, u32[]{:S(2)}, u32[]{:S(2)}) collective-permute-start(bf16[512,768]{1,0:T(8,128)(2,1)} %add_convert_fusion.5), channel_id=1, source_target_pairs={{3,2},{2,1},{7,6},{6,5},{11,10},{10,9},{15,14},{14,13},{19,18},{18... | collective-permute-start | bytes 2359304 | tf_op jit(solution)/shard_map/ppermute | solution.py:864
  329.7 39.2 %collective-permute-start.43 = (bf16[512,768]{1,0:T(8,128)(2,1)}, bf16[512,768]{1,0:T(8,128)(2,1)}, u32[]{:S(2)}, u32[]{:S(2)}) collective-permute-start(bf16[512,768]{1,0:T(8,128)(2,1)} %select_convert_fusion), channel_id=1, source_target_pairs={{0,1},{1,2},{2,3},{4,5},{5,6},{6,7},{8,9},{9,10},{10,11},{12,13},{... | collective-permute-start | bytes 2359304 | tf_op jit(solution)/shard_map/ppermute | solution.py:864
  334.1 34.7 %collective-permute-start.45 = (bf16[512,768]{1,0:T(8,128)(2,1)}, bf16[512,768]{1,0:T(8,128)(2,1)}, u32[]{:S(2)}, u32[]{:S(2)}) collective-permute-start(bf16[512,768]{1,0:T(8,128)(2,1)} %add_convert_fusion.4), channel_id=1, source_target_pairs={{3,2},{2,1},{1,0},{7,6},{6,5},{5,4},{11,10},{10,9},{9,8},{15,14},{... | collective-permute-start | bytes 2359304 | tf_op jit(solution)/shard_map/ppermute | solution.py:864
  380.0 41.6 %collective-permute-start.51 = (bf16[3,4,96,384]{3,2,1,0:T(8,128)(2,1)}, bf16[3,4,96,384]{3,2,1,0:T(8,128)(2,1)}, u32[]{:S(2)}, u32[]{:S(2)}) collective-permute-start(bf16[3,4,96,384]{3,2,1,0:T(8,128)(2,1)} %get-tuple-element.145), channel_id=1, source_target_pairs={{0,4},{4,0},{8,12},{12,8},{16,20},{20,16},{24,28},{28,24},{1,5},{5... | collective-permute-start | bytes 2654216 | tf_op jit(solution)/shard_map/ppermute | solution.py:264
  380.0 41.6 %collective-permute-start.54 = (bf16[3,4,96,384]{3,2,1,0:T(8,128)(2,1)}, bf16[3,4,96,384]{3,2,1,0:T(8,128)(2,1)}, u32[]{:S(2)}, u32[]{:S(2)}) collective-permute-start(bf16[3,4,96,384]{3,2,1,0:T(8,128)(2,1)} %get-tuple-element.144), channel_id=1, source_target_pairs={{0,4},{4,0},{8,12},{12,8},{16,20},{20,16},{24,28},{28,24},{1,5},{5... | collective-permute-start | bytes 2654216 | tf_op jit(solution)/shard_map/ppermute | solution.py:264
  388.1 37.5 %collective-permute-start.61 = (bf16[2,192,768]{2,1,0:T(8,128)(2,1)S(1)}, bf16[2,192,768]{2,1,0:T(8,128)(2,1)S(1)}, u32[]{:S(2)}, u32[]{:S(2)}) collective-permute-start(bf16[2,192,768]{2,1,0:T(8,128)(2,1)S(1)} %copy-done.16), channel_id=1, source_target_pairs={{0,2},{1,3},{2,0},{3,1},{4,6},{5,7},{6,4},{7,5},{8,10},{9,11},{10,... | collective-permute-start | bytes 1769480 | tf_op jit(solution)/shard_map/ppermute | solution.py:264
  391.7 27.0 %collective-permute-start.50 = (f32[20,768]{1,0:T(8,128)S(1)}, f32[20,768]{1,0:T(8,128)S(1)}, u32[]{:S(2)}, u32[]{:S(2)}) collective-permute-start(f32[20,768]{1,0:T(8,128)S(1)} %add.299), channel_id=1, source_target_pairs={{0,2},{1,3},{2,0},{3,1},{4,6},{5,7},{6,4},{7,5},{8,10},{9,11},{10,... | collective-permute-start | bytes 184328 | tf_op jit(solution)/shard_map/ppermute | solution.py:264
  (90 other events, 971.0 us)
